TPU v7x, 512 devices: a whole 4x8x8 slice. The times are simulated.
512 devices in a mesh: lat: 16 (over z, core), lon: 32 (over x, y).
Axes of the slice: x: 4, y: 8, z: 8, core: 2. Of those that a mesh axis runs over, the one named last changes fastest.
Arguments:
- fields: bfloat16 [512, 1024, 256], P('lat', 'lon'), may hold values from -6 to 6
- cotangent: bfloat16 [512, 1024, 256], P('lat', 'lon'), may hold values from -6 to 6
- mix_low: bfloat16 [32, 64, 256, 256], P('lat', 'lon'), may hold values from -6 to 6
- mix_high: bfloat16 [32, 64, 256, 256], P('lat', 'lon'), may hold values from -6 to 6
- point_weight: bfloat16 [256, 256], replicated, may hold values from -0.375 to 0.375
- point_bias: float32 [256], replicated, may hold values from -3 to 3
Outputs:
- field_grad: bfloat16 [512, 1024, 256], P('lat', 'lon')
- mix_low_grad: bfloat16 [32, 64, 256, 256], P('lat', 'lon')
- mix_high_grad: bfloat16 [32, 64, 256, 256], P('lat', 'lon')
- point_weight_grad: float32 [256, 256], replicated
- point_bias_grad: float32 [256], replicated
All inputs are finite; a program needn't handle non-finite values.
Results may differ from a plain program's by a relative error of at most 0.0085.
Values sent between devices are 32-bit elements; how exact they have to be, the bound alone decides.
A program may use at most 64 MiB of HBM per device.

v0:
```python
import math

import jax
import jax.numpy as jnp
from jax import lax
from jax.sharding import PartitionSpec as P

LEVELS = 4


low_taps = (
    -0.010597401784997278,
    0.032883011666982945,
    0.030841381835986965,
    -0.18703481171888114,
    -0.02798376941698385,
    0.6308807679295904,
    0.7148465705525415,
    0.23037781330885523,
)
high_taps = (
    -0.23037781330885523,
    0.7148465705525415,
    -0.6308807679295904,
    -0.02798376941698385,
    0.18703481171888114,
    0.030841381835986965,
    -0.032883011666982945,
    -0.010597401784997278,
)


def with_halo(cells, sides, width, closed):
    for axis, dim in sides:
        count = lax.axis_size(axis)
        ends = count if closed else count - 1
        head = lax.slice_in_dim(cells, 0, width, axis=dim)
        tail = lax.slice_in_dim(cells, cells.shape[dim] - width, cells.shape[dim], axis=dim)
        cells = jnp.concatenate(
            [
                lax.ppermute(tail, axis, [(i, (i + 1) % count) for i in range(ends)]),
                cells,
                lax.ppermute(head, axis, [((i + 1) % count, i) for i in range(ends)]),
            ],
            axis=dim,
        )
    return cells


def lat_edges(field_in, rim_width):
    return with_halo(field_in, (("lat", 1),), rim_width, False)


def lon_edges(field_in, rim_width):
    return with_halo(field_in, (("lon", 2),), rim_width, True)


def reduce_padded(padded, filter_taps, dim_index, count_in):
    result = filter_taps[0] * lax.slice_in_dim(padded, 1, 1 + count_in, 2, dim_index)
    for tap_index in range(1, 8):
        result = result + filter_taps[tap_index] * lax.slice_in_dim(
            padded, tap_index + 1, tap_index + 1 + count_in, 2, dim_index
        )
    return result


def expand_padded(padded, filter_taps, dim_index, count_in):
    even_part = filter_taps[1] * lax.slice_in_dim(padded, 3, 3 + count_in, 1, dim_index)
    odd_part = filter_taps[0] * lax.slice_in_dim(padded, 4, 4 + count_in, 1, dim_index)
    for position in range(1, 4):
        even_part = even_part + filter_taps[2 * position + 1] * lax.slice_in_dim(
            padded, 3 - position, 3 - position + count_in, 1, dim_index
        )
        odd_part = odd_part + filter_taps[2 * position] * lax.slice_in_dim(
            padded, 4 - position, 4 - position + count_in, 1, dim_index
        )
    stacked = jnp.stack([even_part, odd_part], dim_index + 1)
    new_shape = list(even_part.shape)
    new_shape[dim_index] = 2 * count_in
    return stacked.reshape(new_shape)


def level_down(approx, tap_sets):
    row_count = approx.shape[1]
    col_count = approx.shape[2]
    across = reduce_padded(lat_edges(approx, 4), low_taps, 1, row_count)
    padded = lon_edges(across, 4)
    return [reduce_padded(padded, filter_taps, 2, col_count) for filter_taps in tap_sets]


def level_up(stacked, tap_sets):
    row_count = stacked.shape[1]
    col_count = stacked.shape[2]
    padded = lon_edges(stacked, 2)
    widened = expand_padded(padded[0:1], tap_sets[0], 2, col_count)
    for member in range(1, len(tap_sets)):
        widened = widened + expand_padded(
            padded[member : member + 1], tap_sets[member], 2, col_count
        )
    return expand_padded(lat_edges(widened, 2), low_taps, 1, row_count)


def analyse(source):
    approx = source
    for level_index in range(LEVELS - 2):
        approx = level_down(approx, (low_taps,))[0]
    approx = level_down(approx, (low_taps,))[0]
    low_coef, high_coef = level_down(approx, (low_taps, high_taps))
    return (low_coef, high_coef)


def synthesise(low_coef, high_coef):
    approx = level_up(jnp.concatenate([low_coef, high_coef], 0), (low_taps, high_taps))
    approx = level_up(approx, (low_taps,))
    for level_index in range(LEVELS - 2):
        approx = level_up(approx, (low_taps,))
    return approx


def shards(fields, cotangent, mix_low, mix_high, point_weight, point_bias):
    lat_count, lon_count, channels = fields.shape
    source = fields.astype(jnp.float32)[None]
    low_coef, high_coef = analyse(source)
    low_rounded = low_coef.astype(jnp.bfloat16)
    high_rounded = high_coef.astype(jnp.bfloat16)
    mixed_low = jnp.einsum(
        "spqi,pqio->spqo", low_rounded, mix_low, preferred_element_type=jnp.float32
    )
    mixed_high = jnp.einsum(
        "spqi,pqio->spqo", high_rounded, mix_high, preferred_element_type=jnp.float32
    )
    spectral = synthesise(mixed_low, mixed_high)[0]
    flat_fields = fields.reshape(lat_count * lon_count, channels)
    pointwise = jnp.dot(flat_fields, point_weight, preferred_element_type=jnp.float32) + point_bias
    preact = spectral + pointwise.reshape(lat_count, lon_count, channels)
    normal_cdf = 0.5 * (1.0 + lax.erf(preact * (1.0 / math.sqrt(2.0))))
    normal_pdf = jnp.exp(-0.5 * preact * preact) * (1.0 / math.sqrt(2.0 * math.pi))
    grad_pre = cotangent.astype(jnp.float32) * (normal_cdf + preact * normal_pdf)
    grad_rounded = grad_pre.astype(jnp.bfloat16)
    flat_grad = grad_rounded.reshape(lat_count * lon_count, channels)
    weight_part = lax.dot_general(
        flat_fields, flat_grad, (((0,), (0,)), ((), ())), preferred_element_type=jnp.float32
    )
    bias_part = jnp.sum(grad_pre, axis=(0, 1))
    weight_total, bias_total = lax.psum((weight_part, bias_part), ("lat", "lon"))
    grad_scale = 1.0 / math.sqrt(
        lat_count * lax.axis_size("lat") * lon_count * lax.axis_size("lon")
    )
    back_low, back_high = analyse(grad_pre[None])
    mix_low_grad = (
        low_rounded[0].astype(jnp.float32)[:, :, :, None] * back_low[0][:, :, None, :]
    ).astype(jnp.bfloat16)
    mix_high_grad = (
        high_rounded[0].astype(jnp.float32)[:, :, :, None] * back_high[0][:, :, None, :]
    ).astype(jnp.bfloat16)
    pull_low = jnp.einsum(
        "spqo,pqio->spqi",
        back_low.astype(jnp.bfloat16),
        mix_low,
        preferred_element_type=jnp.float32,
    )
    pull_high = jnp.einsum(
        "spqo,pqio->spqi",
        back_high.astype(jnp.bfloat16),
        mix_high,
        preferred_element_type=jnp.float32,
    )
    pulled = synthesise(pull_low, pull_high)[0]
    direct = lax.dot_general(
        flat_grad, point_weight, (((1,), (1,)), ((), ())), preferred_element_type=jnp.float32
    )
    field_grad = (pulled + direct.reshape(lat_count, lon_count, channels)).astype(jnp.bfloat16)
    return (
        field_grad,
        mix_low_grad,
        mix_high_grad,
        weight_total * grad_scale,
        bias_total * grad_scale,
    )


def solution(mesh):
    placed = (
        P("lat", "lon", None),
        P("lat", "lon", None),
        P("lat", "lon", None, None),
        P("lat", "lon", None, None),
        P(),
        P(),
    )
    return jax.shard_map(
        shards,
        mesh=mesh,
        in_specs=placed,
        out_specs=(
            P("lat", "lon", None),
            P("lat", "lon", None, None),
            P("lat", "lon", None, None),
            P(),
            P(),
        ),
        check_vma=False,
    )
```

profile of v0, /device:TPU:1, one launch (start us, length us, event | category | flops | bytes accessed | tf_op | source)
XLA Modules:
  0.0 638.5 jit_solution(17027607359238338774)
XLA Ops:
  8.7 5.4 collective-permute-start
  14.1 4.7 collective-permute-start.1
  22.8 2.2 slice.892
  25.0 2.1 slice.894
  27.1 2.1 slice.895
  29.2 2.1 slice.896
  31.4 2.1 slice.897
  33.4 2.2 multiply_add_fusion.1
  35.6 3.2 collective-permute-start.2
  38.8 6.0 collective-permute-start.3
  46.9 2.0 collective-permute-start.4
  48.9 2.3 collective-permute-start.5
  51.4 3.3 collective-permute-done.5
  57.7 7.2 %collective-permute-start.7 = (f32[1,8,4,256]{3,1,2,0:T(8,128)S(1)}, f32[1,8,4,256]{3,1,2,0:T(8,128)S(1)}, u32[]{:S(2)}, u32[]{:S(2)}) collective-permute-start(f32[1,8,4,256]{3,1,2,0:T(8,128)S(1)} %get-tuple-element.84), channel_id=1, source_target_pairs={{1,0},{2,1},{3,2},{4,3},{5,4},{6,5},{7,6},{8,7},{9,8},{10,9},{11,1... | collective-permute-start | bytes 98312 | tf_op jit(solution)/shard_map/ppermute | solution.py:43
  66.0 2.9 collective-permute-start.8
  70.8 3.3 collective-permute-done.9
  76.3 7.3 %collective-permute-start.11 = (f32[1,4,4,256]{3,1,2,0:T(4,128)S(1)}, f32[1,4,4,256]{3,1,2,0:T(4,128)S(1)}, u32[]{:S(2)}, u32[]{:S(2)}) collective-permute-start(f32[1,4,4,256]{3,1,2,0:T(4,128)S(1)} %get-tuple-element.116), channel_id=1, source_target_pairs={{1,0},{2,1},{3,2},{4,3},{5,4},{6,5},{7,6},{8,7},{9,8},{10,9},{11,1... | collective-permute-start | bytes 49160 | tf_op jit(solution)/shard_map/ppermute | solution.py:43
  84.5 2.8 collective-permute-start.12
  89.3 4.9 collective-permute-done.13
  96.3 6.9 %collective-permute-start.15 = (f32[1,2,4,256]{3,1,2,0:T(2,128)S(1)}, f32[1,2,4,256]{3,1,2,0:T(2,128)S(1)}, u32[]{:S(2)}, u32[]{:S(2)}) collective-permute-start(f32[1,2,4,256]{3,1,2,0:T(2,128)S(1)} %multiply_add_fusion.13), channel_id=1, source_target_pairs={{1,0},{2,1},{3,2},{4,3},{5,4},{6,5},{7,6},{8,7},{9,8},{10,9},{11,1... | collective-permute-start | bytes 24584 | tf_op jit(solution)/shard_map/ppermute | solution.py:43
  104.5 6.9 %collective-permute-start.16 = (f32[2,2,2,256]{3,1,2,0:T(2,128)S(1)}, f32[2,2,2,256]{3,1,2,0:T(2,128)S(1)}, u32[]{:S(2)}, u32[]{:S(2)}) collective-permute-start(f32[2,2,2,256]{3,1,2,0:T(2,128)S(1)} %pad_maximum_fusion.46), channel_id=1, source_target_pairs={{1,0},{2,1},{3,2},{4,3},{5,4},{6,5},{7,6},{8,7},{9,8},{10,9},{11,1... | collective-permute-start | bytes 24584 | tf_op jit(solution)/shard_map/ppermute | solution.py:43
  113.4 5.8 collective-permute-done.17
  121.1 5.2 collective-permute-start.19
  129.2 6.7 %collective-permute-start.20 = (f32[1,4,2,256]{3,1,2,0:T(4,128)S(1)}, f32[1,4,2,256]{3,1,2,0:T(4,128)S(1)}, u32[]{:S(2)}, u32[]{:S(2)}) collective-permute-start(f32[1,4,2,256]{3,1,2,0:T(4,128)S(1)} %copy.141), channel_id=1, source_target_pairs={{1,0},{2,1},{3,2},{4,3},{5,4},{6,5},{7,6},{8,7},{9,8},{10,9},{11,1... | collective-permute-start | bytes 24584 | tf_op jit(solution)/shard_map/ppermute | solution.py:43
  138.6 5.3 collective-permute-start.23
  146.9 7.2 %collective-permute-start.24 = (f32[1,8,2,256]{3,1,2,0:T(8,128)S(1)}, f32[1,8,2,256]{3,1,2,0:T(8,128)S(1)}, u32[]{:S(2)}, u32[]{:S(2)}) collective-permute-start(f32[1,8,2,256]{3,1,2,0:T(8,128)S(1)} %copy.143), channel_id=1, source_target_pairs={{1,0},{2,1},{3,2},{4,3},{5,4},{6,5},{7,6},{8,7},{9,8},{10,9},{11,1... | collective-permute-start | bytes 49160 | tf_op jit(solution)/shard_map/ppermute | solution.py:43
  157.1 5.1 collective-permute-start.27
  165.4 7.2 %collective-permute-start.28 = (f32[1,16,2,256]{3,1,2,0:T(8,128)S(1)}, f32[1,16,2,256]{3,1,2,0:T(8,128)S(1)}, u32[]{:S(2)}, u32[]{:S(2)}) collective-permute-start(f32[1,16,2,256]{3,1,2,0:T(8,128)S(1)} %copy.145), channel_id=1, source_target_pairs={{1,0},{2,1},{3,2},{4,3},{5,4},{6,5},{7,6},{8,7},{9,8},{10,9},{11,1... | collective-permute-start | bytes 98312 | tf_op jit(solution)/shard_map/ppermute | solution.py:43
  174.1 2.1 collective-permute-start.30
  176.2 5.1 collective-permute-start.31
  185.9 4.3 collective-permute-start.32
  190.2 2.1 collective-permute-start.33
  193.6 3.0 collective-permute-done.33
  197.8 2.1 slice.1012
  199.9 2.1 slice.1013
  202.0 2.1 slice.1014
  204.1 2.1 slice.1016
  206.3 2.1 slice.1017
  208.4 2.1 slice.1018
  210.5 2.1 slice.1019
  212.6 2.5 multiply_add_fusion
  217.1 7.3 %collective-permute-start.35 = (f32[1,16,4,256]{3,1,2,0:T(8,128)S(1)}, f32[1,16,4,256]{3,1,2,0:T(8,128)S(1)}, u32[]{:S(2)}, u32[]{:S(2)}) collective-permute-start(f32[1,16,4,256]{3,1,2,0:T(8,128)S(1)} %get-tuple-element.52), channel_id=1, source_target_pairs={{1,0},{2,1},{3,2},{4,3},{5,4},{6,5},{7,6},{8,7},{9,8},{10,9},{11,1... | collective-permute-start | bytes 196616 | tf_op jit(solution)/shard_map/ppermute | solution.py:43
  225.9 3.3 collective-permute-start.36
  231.3 4.5 collective-permute-done.37
  238.7 7.0 %collective-permute-start.39 = (f32[1,8,4,256]{3,1,2,0:T(8,128)S(1)}, f32[1,8,4,256]{3,1,2,0:T(8,128)S(1)}, u32[]{:S(2)}, u32[]{:S(2)}) collective-permute-start(f32[1,8,4,256]{3,1,2,0:T(8,128)S(1)} %get-tuple-element.80), channel_id=1, source_target_pairs={{1,0},{2,1},{3,2},{4,3},{5,4},{6,5},{7,6},{8,7},{9,8},{10,9},{11,1... | collective-permute-start | bytes 98312 | tf_op jit(solution)/shard_map/ppermute | solution.py:43
  246.9 3.4 collective-permute-start.40
  252.2 7.7 %collective-permute-done.41 = f32[1,4,8,256]{3,1,2,0:T(4,128)S(1)} collective-permute-done((f32[1,4,8,256]{3,1,2,0:T(4,128)S(1)}, f32[1,4,8,256]{3,1,2,0:T(4,128)S(1)}, u32[]{:S(2)}, u32[]{:S(2)}) %collective-permute-start.41) | collective-permute-done | bytes 32800 | tf_op jit(solution)/shard_map/ppermute | solution.py:43
  262.2 7.0 %collective-permute-start.43 = (f32[1,4,4,256]{3,1,2,0:T(4,128)S(1)}, f32[1,4,4,256]{3,1,2,0:T(4,128)S(1)}, u32[]{:S(2)}, u32[]{:S(2)}) collective-permute-start(f32[1,4,4,256]{3,1,2,0:T(4,128)S(1)} %get-tuple-element.112), channel_id=1, source_target_pairs={{1,0},{2,1},{3,2},{4,3},{5,4},{6,5},{7,6},{8,7},{9,8},{10,9},{11,1... | collective-permute-start | bytes 49160 | tf_op jit(solution)/shard_map/ppermute | solution.py:43
  270.1 4.7 collective-permute-start.44
  276.7 5.0 collective-permute-done.45
  283.9 6.9 %collective-permute-start.47 = (f32[1,2,4,256]{3,1,2,0:T(2,128)S(1)}, f32[1,2,4,256]{3,1,2,0:T(2,128)S(1)}, u32[]{:S(2)}, u32[]{:S(2)}) collective-permute-start(f32[1,2,4,256]{3,1,2,0:T(2,128)S(1)} %multiply_add_fusion.12), channel_id=1, source_target_pairs={{1,0},{2,1},{3,2},{4,3},{5,4},{6,5},{7,6},{8,7},{9,8},{10,9},{11,1... | collective-permute-start | bytes 24584 | tf_op jit(solution)/shard_map/ppermute | solution.py:43
  292.2 7.1 %collective-permute-start.48 = (f32[2,2,2,256]{3,1,2,0:T(2,128)S(1)}, f32[2,2,2,256]{3,1,2,0:T(2,128)S(1)}, u32[]{:S(2)}, u32[]{:S(2)}) collective-permute-start(f32[2,2,2,256]{3,1,2,0:T(2,128)S(1)} %pad_maximum_fusion.47), channel_id=1, source_target_pairs={{1,0},{2,1},{3,2},{4,3},{5,4},{6,5},{7,6},{8,7},{9,8},{10,9},{11,1... | collective-permute-start | bytes 24584 | tf_op jit(solution)/shard_map/ppermute | solution.py:43
  301.2 5.8 collective-permute-done.49
  309.0 5.1 collective-permute-start.51
  317.1 6.7 %collective-permute-start.52 = (f32[1,4,2,256]{3,1,2,0:T(4,128)S(1)}, f32[1,4,2,256]{3,1,2,0:T(4,128)S(1)}, u32[]{:S(2)}, u32[]{:S(2)}) collective-permute-start(f32[1,4,2,256]{3,1,2,0:T(4,128)S(1)} %copy.147), channel_id=1, source_target_pairs={{1,0},{2,1},{3,2},{4,3},{5,4},{6,5},{7,6},{8,7},{9,8},{10,9},{11,1... | collective-permute-start | bytes 24584 | tf_op jit(solution)/shard_map/ppermute | solution.py:43
  326.5 5.3 collective-permute-start.55
  333.1 107.0 %psum.15 = f32[256]{0:T(256)S(1)} all-reduce(f32[256]{0:T(256)S(1)} %get-tuple-element.15), channel_id=1, replica_groups=mesh['lat'=16,'lon'=32] {'lat','lon'}, use_global_device_ids=true, to_apply=%region_2.0 | all-reduce | flops 256 | bytes 2048 | tf_op jit(solution)/shard_map/psum | solution.py:145
  442.8 6.7 %collective-permute-start.56 = (f32[1,8,2,256]{3,1,2,0:T(8,128)S(1)}, f32[1,8,2,256]{3,1,2,0:T(8,128)S(1)}, u32[]{:S(2)}, u32[]{:S(2)}) collective-permute-start(f32[1,8,2,256]{3,1,2,0:T(8,128)S(1)} %copy.149), channel_id=1, source_target_pairs={{1,0},{2,1},{3,2},{4,3},{5,4},{6,5},{7,6},{8,7},{9,8},{10,9},{11,1... | collective-permute-start | bytes 49160 | tf_op jit(solution)/shard_map/ppermute | solution.py:43
  450.4 3.8 collective-permute-start.58
  456.2 152.7 %all-reduce.2.cloned.1.call-done = f32[256,256]{0,1:T(8,128)} async-done(((f32[256,256]{0,1:T(8,128)}), f32[256,256]{0,1:T(8,128)}) %all-reduce.2.cloned.1.call-update) | async-done | bytes 262160 | tf_op jit(solution)/shard_map/psum | solution.py:145
  611.1 3.0 collective-permute-start.61
  615.1 5.6 collective-permute-start.60
  622.3 2.3 collective-permute-start.62
  624.7 3.2 collective-permute-start.63
  (310 shorter events, 93.3 us)
Async XLA Ops:
  7.2 601.8 %all-reduce.2.cloned.1.call-start = ((), (), s32[]{:S(2)}) async-start(), calls=%async_computation | async-start | bytes 524288 | tf_op jit(solution)/shard_map/psum | solution.py:145
  8.7 10.7 %collective-permute-start = (f32[1,4,32,256]{3,1,2,0:T(4,128)S(1)}, f32[1,4,32,256]{3,1,2,0:T(4,128)S(1)}, u32[]{:S(2)}, u32[]{:S(2)}) collective-permute-start(f32[1,4,32,256]{3,1,2,0:T(4,128)S(1)} %get-tuple-element.39), channel_id=1, source_target_pairs={{0,32},{32,64},{64,96},{96,128},{128,160},{160,192},{192,224},{224... | collective-permute-start | bytes 393224 | tf_op jit(solution)/shard_map/ppermute | solution.py:41
  14.1 6.4 %collective-permute-start.1 = (f32[1,4,32,256]{3,1,2,0:T(4,128)S(1)}, f32[1,4,32,256]{3,1,2,0:T(4,128)}, u32[]{:S(2)}, u32[]{:S(2)}) collective-permute-start(f32[1,4,32,256]{3,1,2,0:T(4,128)S(1)} %get-tuple-element.40), channel_id=1, source_target_pairs={{32,0},{64,32},{96,64},{128,96},{160,128},{192,160},{224,192},{256... | collective-permute-start | bytes 393224 | tf_op jit(solution)/shard_map/ppermute | solution.py:43
  35.6 9.2 %collective-permute-start.2 = (f32[1,16,4,256]{3,1,2,0:T(8,128)S(1)}, f32[1,16,4,256]{3,1,2,0:T(8,128)S(1)}, u32[]{:S(2)}, u32[]{:S(2)}) collective-permute-start(f32[1,16,4,256]{3,1,2,0:T(8,128)S(1)} %get-tuple-element.55), channel_id=1, source_target_pairs={{0,1},{1,2},{2,3},{3,4},{4,5},{5,6},{6,7},{7,8},{8,9},{9,10},{10,1... | collective-permute-start | bytes 196616 | tf_op jit(solution)/shard_map/ppermute | solution.py:41
  38.8 7.9 %collective-permute-start.3 = (f32[1,16,4,256]{3,1,2,0:T(8,128)S(1)}, f32[1,16,4,256]{3,1,2,0:T(8,128)S(1)}, u32[]{:S(2)}, u32[]{:S(2)}) collective-permute-start(f32[1,16,4,256]{3,1,2,0:T(8,128)S(1)} %get-tuple-element.56), channel_id=1, source_target_pairs={{1,0},{2,1},{3,2},{4,3},{5,4},{6,5},{7,6},{8,7},{9,8},{10,9},{11,1... | collective-permute-start | bytes 196616 | tf_op jit(solution)/shard_map/ppermute | solution.py:43
  48.9 5.7 collective-permute-start.5
  55.7 9.1 %collective-permute-start.6 = (f32[1,8,4,256]{3,1,2,0:T(8,128)S(1)}, f32[1,8,4,256]{3,1,2,0:T(8,128)S(1)}, u32[]{:S(2)}, u32[]{:S(2)}) collective-permute-start(f32[1,8,4,256]{3,1,2,0:T(8,128)S(1)} %get-tuple-element.83), channel_id=1, source_target_pairs={{0,1},{1,2},{2,3},{3,4},{4,5},{5,6},{6,7},{7,8},{8,9},{9,10},{10,1... | collective-permute-start | bytes 98312 | tf_op jit(solution)/shard_map/ppermute | solution.py:41
  57.7 8.2 %collective-permute-start.7 = (f32[1,8,4,256]{3,1,2,0:T(8,128)S(1)}, f32[1,8,4,256]{3,1,2,0:T(8,128)S(1)}, u32[]{:S(2)}, u32[]{:S(2)}) collective-permute-start(f32[1,8,4,256]{3,1,2,0:T(8,128)S(1)} %get-tuple-element.84), channel_id=1, source_target_pairs={{1,0},{2,1},{3,2},{4,3},{5,4},{6,5},{7,6},{8,7},{9,8},{10,9},{11,1... | collective-permute-start | bytes 98312 | tf_op jit(solution)/shard_map/ppermute | solution.py:43
  66.0 4.8 collective-permute-start.8
  68.8 5.2 collective-permute-start.9
  74.4 9.2 %collective-permute-start.10 = (f32[1,4,4,256]{3,1,2,0:T(4,128)S(1)}, f32[1,4,4,256]{3,1,2,0:T(4,128)S(1)}, u32[]{:S(2)}, u32[]{:S(2)}) collective-permute-start(f32[1,4,4,256]{3,1,2,0:T(4,128)S(1)} %get-tuple-element.115), channel_id=1, source_target_pairs={{0,1},{1,2},{2,3},{3,4},{4,5},{5,6},{6,7},{7,8},{8,9},{9,10},{10,1... | collective-permute-start | bytes 49160 | tf_op jit(solution)/shard_map/ppermute | solution.py:41
  76.3 8.1 %collective-permute-start.11 = (f32[1,4,4,256]{3,1,2,0:T(4,128)S(1)}, f32[1,4,4,256]{3,1,2,0:T(4,128)S(1)}, u32[]{:S(2)}, u32[]{:S(2)}) collective-permute-start(f32[1,4,4,256]{3,1,2,0:T(4,128)S(1)} %get-tuple-element.116), channel_id=1, source_target_pairs={{1,0},{2,1},{3,2},{4,3},{5,4},{6,5},{7,6},{8,7},{9,8},{10,9},{11,1... | collective-permute-start | bytes 49160 | tf_op jit(solution)/shard_map/ppermute | solution.py:43
  84.5 4.7 collective-permute-start.12
  87.3 6.9 %collective-permute-start.13 = (f32[1,4,4,256]{3,1,2,0:T(4,128)S(1)}, f32[1,4,4,256]{3,1,2,0:T(4,128)S(1)}, u32[]{:S(2)}, u32[]{:S(2)}) collective-permute-start(f32[1,4,4,256]{3,1,2,0:T(4,128)S(1)} %multiply_add_fusion.11), channel_id=1, source_target_pairs={{32,0},{64,32},{96,64},{128,96},{160,128},{192,160},{224,192},{256... | collective-permute-start | bytes 49160 | tf_op jit(solution)/shard_map/ppermute | solution.py:43
  94.4 8.9 %collective-permute-start.14 = (f32[1,2,4,256]{3,1,2,0:T(2,128)S(1)}, f32[1,2,4,256]{3,1,2,0:T(2,128)S(1)}, u32[]{:S(2)}, u32[]{:S(2)}) collective-permute-start(f32[1,2,4,256]{3,1,2,0:T(2,128)S(1)} %multiply_add_fusion.13), channel_id=1, source_target_pairs={{0,1},{1,2},{2,3},{3,4},{4,5},{5,6},{6,7},{7,8},{8,9},{9,10},{10,1... | collective-permute-start | bytes 24584 | tf_op jit(solution)/shard_map/ppermute | solution.py:41
  96.3 7.7 %collective-permute-start.15 = (f32[1,2,4,256]{3,1,2,0:T(2,128)S(1)}, f32[1,2,4,256]{3,1,2,0:T(2,128)S(1)}, u32[]{:S(2)}, u32[]{:S(2)}) collective-permute-start(f32[1,2,4,256]{3,1,2,0:T(2,128)S(1)} %multiply_add_fusion.13), channel_id=1, source_target_pairs={{1,0},{2,1},{3,2},{4,3},{5,4},{6,5},{7,6},{8,7},{9,8},{10,9},{11,1... | collective-permute-start | bytes 24584 | tf_op jit(solution)/shard_map/ppermute | solution.py:43
  104.5 8.9 %collective-permute-start.16 = (f32[2,2,2,256]{3,1,2,0:T(2,128)S(1)}, f32[2,2,2,256]{3,1,2,0:T(2,128)S(1)}, u32[]{:S(2)}, u32[]{:S(2)}) collective-permute-start(f32[2,2,2,256]{3,1,2,0:T(2,128)S(1)} %pad_maximum_fusion.46), channel_id=1, source_target_pairs={{1,0},{2,1},{3,2},{4,3},{5,4},{6,5},{7,6},{8,7},{9,8},{10,9},{11,1... | collective-permute-start | bytes 24584 | tf_op jit(solution)/shard_map/ppermute | solution.py:43
  111.4 7.7 %collective-permute-start.17 = (f32[2,2,2,256]{3,1,2,0:T(2,128)S(1)}, f32[2,2,2,256]{3,1,2,0:T(2,128)S(1)}, u32[]{:S(2)}, u32[]{:S(2)}) collective-permute-start(f32[2,2,2,256]{3,1,2,0:T(2,128)S(1)} %pad_maximum_fusion.46), channel_id=1, source_target_pairs={{0,1},{1,2},{2,3},{3,4},{4,5},{5,6},{6,7},{7,8},{8,9},{9,10},{10,1... | collective-permute-start | bytes 24584 | tf_op jit(solution)/shard_map/ppermute | solution.py:41
  119.2 7.1 %collective-permute-start.18 = (f32[1,2,4,256]{3,1,2,0:T(2,128)S(1)}, f32[1,2,4,256]{3,1,2,0:T(2,128)S(1)}, u32[]{:S(2)}, u32[]{:S(2)}) collective-permute-start(f32[1,2,4,256]{3,1,2,0:T(2,128)S(1)} %bitcast.249), channel_id=1, source_target_pairs={{32,0},{64,32},{96,64},{128,96},{160,128},{192,160},{224,192},{256... | collective-permute-start | bytes 24584 | tf_op jit(solution)/shard_map/ppermute | solution.py:43
  121.1 6.0 collective-permute-start.19
  127.2 8.6 %collective-permute-start.21 = (f32[1,4,2,256]{3,1,2,0:T(4,128)S(1)}, f32[1,4,2,256]{3,1,2,0:T(4,128)S(1)}, u32[]{:S(2)}, u32[]{:S(2)}) collective-permute-start(f32[1,4,2,256]{3,1,2,0:T(4,128)S(1)} %copy.142), channel_id=1, source_target_pairs={{0,1},{1,2},{2,3},{3,4},{4,5},{5,6},{6,7},{7,8},{8,9},{9,10},{10,1... | collective-permute-start | bytes 24584 | tf_op jit(solution)/shard_map/ppermute | solution.py:41
  129.2 7.5 %collective-permute-start.20 = (f32[1,4,2,256]{3,1,2,0:T(4,128)S(1)}, f32[1,4,2,256]{3,1,2,0:T(4,128)S(1)}, u32[]{:S(2)}, u32[]{:S(2)}) collective-permute-start(f32[1,4,2,256]{3,1,2,0:T(4,128)S(1)} %copy.141), channel_id=1, source_target_pairs={{1,0},{2,1},{3,2},{4,3},{5,4},{6,5},{7,6},{8,7},{9,8},{10,9},{11,1... | collective-permute-start | bytes 24584 | tf_op jit(solution)/shard_map/ppermute | solution.py:43
  136.7 7.3 %collective-permute-start.22 = (f32[1,2,8,256]{3,1,2,0:T(2,128)S(1)}, f32[1,2,8,256]{3,1,2,0:T(2,128)S(1)}, u32[]{:S(2)}, u32[]{:S(2)}) collective-permute-start(f32[1,2,8,256]{3,1,2,0:T(2,128)S(1)} %get-tuple-element.114), channel_id=1, source_target_pairs={{32,0},{64,32},{96,64},{128,96},{160,128},{192,160},{224,192},{256... | collective-permute-start | bytes 49160 | tf_op jit(solution)/shard_map/ppermute | solution.py:43
  138.6 6.2 collective-permute-start.23
  145.0 9.2 %collective-permute-start.25 = (f32[1,8,2,256]{3,1,2,0:T(8,128)S(1)}, f32[1,8,2,256]{3,1,2,0:T(8,128)S(1)}, u32[]{:S(2)}, u32[]{:S(2)}) collective-permute-start(f32[1,8,2,256]{3,1,2,0:T(8,128)S(1)} %copy.144), channel_id=1, source_target_pairs={{0,1},{1,2},{2,3},{3,4},{4,5},{5,6},{6,7},{7,8},{8,9},{9,10},{10,1... | collective-permute-start | bytes 49160 | tf_op jit(solution)/shard_map/ppermute | solution.py:41
  146.9 8.1 %collective-permute-start.24 = (f32[1,8,2,256]{3,1,2,0:T(8,128)S(1)}, f32[1,8,2,256]{3,1,2,0:T(8,128)S(1)}, u32[]{:S(2)}, u32[]{:S(2)}) collective-permute-start(f32[1,8,2,256]{3,1,2,0:T(8,128)S(1)} %copy.143), channel_id=1, source_target_pairs={{1,0},{2,1},{3,2},{4,3},{5,4},{6,5},{7,6},{8,7},{9,8},{10,9},{11,1... | collective-permute-start | bytes 49160 | tf_op jit(solution)/shard_map/ppermute | solution.py:43
  155.2 7.0 %collective-permute-start.26 = (f32[1,2,16,256]{3,1,2,0:T(2,128)S(1)}, f32[1,2,16,256]{3,1,2,0:T(2,128)S(1)}, u32[]{:S(2)}, u32[]{:S(2)}) collective-permute-start(f32[1,2,16,256]{3,1,2,0:T(2,128)S(1)} %get-tuple-element.82), channel_id=1, source_target_pairs={{32,0},{64,32},{96,64},{128,96},{160,128},{192,160},{224,192},{256... | collective-permute-start | bytes 98312 | tf_op jit(solution)/shard_map/ppermute | solution.py:43
  157.1 6.1 collective-permute-start.27
  163.5 9.2 %collective-permute-start.29 = (f32[1,16,2,256]{3,1,2,0:T(8,128)S(1)}, f32[1,16,2,256]{3,1,2,0:T(8,128)S(1)}, u32[]{:S(2)}, u32[]{:S(2)}) collective-permute-start(f32[1,16,2,256]{3,1,2,0:T(8,128)S(1)} %copy.146), channel_id=1, source_target_pairs={{0,1},{1,2},{2,3},{3,4},{4,5},{5,6},{6,7},{7,8},{8,9},{9,10},{10,1... | collective-permute-start | bytes 98312 | tf_op jit(solution)/shard_map/ppermute | solution.py:41
  165.4 8.3 %collective-permute-start.28 = (f32[1,16,2,256]{3,1,2,0:T(8,128)S(1)}, f32[1,16,2,256]{3,1,2,0:T(8,128)S(1)}, u32[]{:S(2)}, u32[]{:S(2)}) collective-permute-start(f32[1,16,2,256]{3,1,2,0:T(8,128)S(1)} %copy.145), channel_id=1, source_target_pairs={{1,0},{2,1},{3,2},{4,3},{5,4},{6,5},{7,6},{8,7},{9,8},{10,9},{11,1... | collective-permute-start | bytes 98312 | tf_op jit(solution)/shard_map/ppermute | solution.py:43
  174.1 7.5 %collective-permute-start.30 = (f32[1,2,32,256]{3,1,2,0:T(2,128)S(1)}, f32[1,2,32,256]{3,1,2,0:T(2,128)S(1)}, u32[]{:S(2)}, u32[]{:S(2)}) collective-permute-start(f32[1,2,32,256]{3,1,2,0:T(2,128)S(1)} %get-tuple-element.54), channel_id=1, source_target_pairs={{32,0},{64,32},{96,64},{128,96},{160,128},{192,160},{224,192},{256... | collective-permute-start | bytes 196616 | tf_op jit(solution)/shard_map/ppermute | solution.py:43
  176.2 6.4 %collective-permute-start.31 = (f32[1,2,32,256]{3,1,2,0:T(2,128)S(1)}, f32[1,2,32,256]{3,1,2,0:T(2,128)S(1)}, u32[]{:S(2)}, u32[]{:S(2)}) collective-permute-start(f32[1,2,32,256]{3,1,2,0:T(2,128)S(1)} %get-tuple-element.53), channel_id=1, source_target_pairs={{0,32},{32,64},{64,96},{96,128},{128,160},{160,192},{192,224},{224... | collective-permute-start | bytes 196616 | tf_op jit(solution)/shard_map/ppermute | solution.py:41
  185.9 7.0 %collective-permute-start.32 = (f32[1,4,32,256]{3,1,2,0:T(4,128)S(1)}, f32[1,4,32,256]{3,1,2,0:T(4,128)S(1)}, u32[]{:S(2)}, u32[]{:S(2)}) collective-permute-start(f32[1,4,32,256]{3,1,2,0:T(4,128)S(1)} %get-tuple-element.37), channel_id=1, source_target_pairs={{0,32},{32,64},{64,96},{96,128},{128,160},{160,192},{192,224},{224... | collective-permute-start | bytes 393224 | tf_op jit(solution)/shard_map/ppermute | solution.py:41
  190.2 6.4 %collective-permute-start.33 = (f32[1,4,32,256]{3,1,2,0:T(4,128)S(1)}, f32[1,4,32,256]{3,1,2,0:T(4,128)}, u32[]{:S(2)}, u32[]{:S(2)}) collective-permute-start(f32[1,4,32,256]{3,1,2,0:T(4,128)S(1)} %get-tuple-element.38), channel_id=1, source_target_pairs={{32,0},{64,32},{96,64},{128,96},{160,128},{192,160},{224,192},{256... | collective-permute-start | bytes 393224 | tf_op jit(solution)/shard_map/ppermute | solution.py:43
  215.1 9.2 %collective-permute-start.34 = (f32[1,16,4,256]{3,1,2,0:T(8,128)S(1)}, f32[1,16,4,256]{3,1,2,0:T(8,128)S(1)}, u32[]{:S(2)}, u32[]{:S(2)}) collective-permute-start(f32[1,16,4,256]{3,1,2,0:T(8,128)S(1)} %get-tuple-element.51), channel_id=1, source_target_pairs={{0,1},{1,2},{2,3},{3,4},{4,5},{5,6},{6,7},{7,8},{8,9},{9,10},{10,1... | collective-permute-start | bytes 196616 | tf_op jit(solution)/shard_map/ppermute | solution.py:41
  217.1 8.6 %collective-permute-start.35 = (f32[1,16,4,256]{3,1,2,0:T(8,128)S(1)}, f32[1,16,4,256]{3,1,2,0:T(8,128)S(1)}, u32[]{:S(2)}, u32[]{:S(2)}) collective-permute-start(f32[1,16,4,256]{3,1,2,0:T(8,128)S(1)} %get-tuple-element.52), channel_id=1, source_target_pairs={{1,0},{2,1},{3,2},{4,3},{5,4},{6,5},{7,6},{8,7},{9,8},{10,9},{11,1... | collective-permute-start | bytes 196616 | tf_op jit(solution)/shard_map/ppermute | solution.py:43
  225.9 5.4 collective-permute-start.36
  229.2 6.5 %collective-permute-start.37 = (f32[1,4,16,256]{3,1,2,0:T(4,128)S(1)}, f32[1,4,16,256]{3,1,2,0:T(4,128)S(1)}, u32[]{:S(2)}, u32[]{:S(2)}) collective-permute-start(f32[1,4,16,256]{3,1,2,0:T(4,128)S(1)} %get-tuple-element.62), channel_id=1, source_target_pairs={{32,0},{64,32},{96,64},{128,96},{160,128},{192,160},{224,192},{256... | collective-permute-start | bytes 196616 | tf_op jit(solution)/shard_map/ppermute | solution.py:43
  236.8 9.0 %collective-permute-start.38 = (f32[1,8,4,256]{3,1,2,0:T(8,128)S(1)}, f32[1,8,4,256]{3,1,2,0:T(8,128)S(1)}, u32[]{:S(2)}, u32[]{:S(2)}) collective-permute-start(f32[1,8,4,256]{3,1,2,0:T(8,128)S(1)} %get-tuple-element.79), channel_id=1, source_target_pairs={{0,1},{1,2},{2,3},{3,4},{4,5},{5,6},{6,7},{7,8},{8,9},{9,10},{10,1... | collective-permute-start | bytes 98312 | tf_op jit(solution)/shard_map/ppermute | solution.py:41
  238.7 8.0 %collective-permute-start.39 = (f32[1,8,4,256]{3,1,2,0:T(8,128)S(1)}, f32[1,8,4,256]{3,1,2,0:T(8,128)S(1)}, u32[]{:S(2)}, u32[]{:S(2)}) collective-permute-start(f32[1,8,4,256]{3,1,2,0:T(8,128)S(1)} %get-tuple-element.80), channel_id=1, source_target_pairs={{1,0},{2,1},{3,2},{4,3},{5,4},{6,5},{7,6},{8,7},{9,8},{10,9},{11,1... | collective-permute-start | bytes 98312 | tf_op jit(solution)/shard_map/ppermute | solution.py:43
  246.9 5.4 collective-permute-start.40
  250.3 9.7 %collective-permute-start.41 = (f32[1,4,8,256]{3,1,2,0:T(4,128)S(1)}, f32[1,4,8,256]{3,1,2,0:T(4,128)S(1)}, u32[]{:S(2)}, u32[]{:S(2)}) collective-permute-start(f32[1,4,8,256]{3,1,2,0:T(4,128)S(1)} %get-tuple-element.94), channel_id=1, source_target_pairs={{32,0},{64,32},{96,64},{128,96},{160,128},{192,160},{224,192},{256... | collective-permute-start | bytes 98312 | tf_op jit(solution)/shard_map/ppermute | solution.py:43
  260.3 8.9 %collective-permute-start.42 = (f32[1,4,4,256]{3,1,2,0:T(4,128)S(1)}, f32[1,4,4,256]{3,1,2,0:T(4,128)S(1)}, u32[]{:S(2)}, u32[]{:S(2)}) collective-permute-start(f32[1,4,4,256]{3,1,2,0:T(4,128)S(1)} %get-tuple-element.111), channel_id=1, source_target_pairs={{0,1},{1,2},{2,3},{3,4},{4,5},{5,6},{6,7},{7,8},{8,9},{9,10},{10,1... | collective-permute-start | bytes 49160 | tf_op jit(solution)/shard_map/ppermute | solution.py:41
  262.2 7.8 %collective-permute-start.43 = (f32[1,4,4,256]{3,1,2,0:T(4,128)S(1)}, f32[1,4,4,256]{3,1,2,0:T(4,128)S(1)}, u32[]{:S(2)}, u32[]{:S(2)}) collective-permute-start(f32[1,4,4,256]{3,1,2,0:T(4,128)S(1)} %get-tuple-element.112), channel_id=1, source_target_pairs={{1,0},{2,1},{3,2},{4,3},{5,4},{6,5},{7,6},{8,7},{9,8},{10,9},{11,1... | collective-permute-start | bytes 49160 | tf_op jit(solution)/shard_map/ppermute | solution.py:43
  270.1 6.6 %collective-permute-start.44 = (f32[1,4,4,256]{3,1,2,0:T(4,128)S(1)}, f32[1,4,4,256]{3,1,2,0:T(4,128)S(1)}, u32[]{:S(2)}, u32[]{:S(2)}) collective-permute-start(f32[1,4,4,256]{3,1,2,0:T(4,128)S(1)} %multiply_add_fusion.10), channel_id=1, source_target_pairs={{0,32},{32,64},{64,96},{96,128},{128,160},{160,192},{192,224},{224... | collective-permute-start | bytes 49160 | tf_op jit(solution)/shard_map/ppermute | solution.py:41
  274.8 7.0 %collective-permute-start.45 = (f32[1,4,4,256]{3,1,2,0:T(4,128)S(1)}, f32[1,4,4,256]{3,1,2,0:T(4,128)S(1)}, u32[]{:S(2)}, u32[]{:S(2)}) collective-permute-start(f32[1,4,4,256]{3,1,2,0:T(4,128)S(1)} %multiply_add_fusion.10), channel_id=1, source_target_pairs={{32,0},{64,32},{96,64},{128,96},{160,128},{192,160},{224,192},{256... | collective-permute-start | bytes 49160 | tf_op jit(solution)/shard_map/ppermute | solution.py:43
  282.0 8.9 %collective-permute-start.46 = (f32[1,2,4,256]{3,1,2,0:T(2,128)S(1)}, f32[1,2,4,256]{3,1,2,0:T(2,128)S(1)}, u32[]{:S(2)}, u32[]{:S(2)}) collective-permute-start(f32[1,2,4,256]{3,1,2,0:T(2,128)S(1)} %multiply_add_fusion.12), channel_id=1, source_target_pairs={{0,1},{1,2},{2,3},{3,4},{4,5},{5,6},{6,7},{7,8},{8,9},{9,10},{10,1... | collective-permute-start | bytes 24584 | tf_op jit(solution)/shard_map/ppermute | solution.py:41
  283.9 7.7 %collective-permute-start.47 = (f32[1,2,4,256]{3,1,2,0:T(2,128)S(1)}, f32[1,2,4,256]{3,1,2,0:T(2,128)S(1)}, u32[]{:S(2)}, u32[]{:S(2)}) collective-permute-start(f32[1,2,4,256]{3,1,2,0:T(2,128)S(1)} %multiply_add_fusion.12), channel_id=1, source_target_pairs={{1,0},{2,1},{3,2},{4,3},{5,4},{6,5},{7,6},{8,7},{9,8},{10,9},{11,1... | collective-permute-start | bytes 24584 | tf_op jit(solution)/shard_map/ppermute | solution.py:43
  292.2 9.0 %collective-permute-start.48 = (f32[2,2,2,256]{3,1,2,0:T(2,128)S(1)}, f32[2,2,2,256]{3,1,2,0:T(2,128)S(1)}, u32[]{:S(2)}, u32[]{:S(2)}) collective-permute-start(f32[2,2,2,256]{3,1,2,0:T(2,128)S(1)} %pad_maximum_fusion.47), channel_id=1, source_target_pairs={{1,0},{2,1},{3,2},{4,3},{5,4},{6,5},{7,6},{8,7},{9,8},{10,9},{11,1... | collective-permute-start | bytes 24584 | tf_op jit(solution)/shard_map/ppermute | solution.py:43
  299.3 7.7 %collective-permute-start.49 = (f32[2,2,2,256]{3,1,2,0:T(2,128)S(1)}, f32[2,2,2,256]{3,1,2,0:T(2,128)S(1)}, u32[]{:S(2)}, u32[]{:S(2)}) collective-permute-start(f32[2,2,2,256]{3,1,2,0:T(2,128)S(1)} %pad_maximum_fusion.47), channel_id=1, source_target_pairs={{0,1},{1,2},{2,3},{3,4},{4,5},{5,6},{6,7},{7,8},{8,9},{9,10},{10,1... | collective-permute-start | bytes 24584 | tf_op jit(solution)/shard_map/ppermute | solution.py:41
  307.1 7.0 %collective-permute-start.50 = (f32[1,2,4,256]{3,1,2,0:T(2,128)S(1)}, f32[1,2,4,256]{3,1,2,0:T(2,128)S(1)}, u32[]{:S(2)}, u32[]{:S(2)}) collective-permute-start(f32[1,2,4,256]{3,1,2,0:T(2,128)S(1)} %bitcast.252), channel_id=1, source_target_pairs={{32,0},{64,32},{96,64},{128,96},{160,128},{192,160},{224,192},{256... | collective-permute-start | bytes 24584 | tf_op jit(solution)/shard_map/ppermute | solution.py:43
  309.0 5.9 collective-permute-start.51
  315.0 8.7 %collective-permute-start.53 = (f32[1,4,2,256]{3,1,2,0:T(4,128)S(1)}, f32[1,4,2,256]{3,1,2,0:T(4,128)S(1)}, u32[]{:S(2)}, u32[]{:S(2)}) collective-permute-start(f32[1,4,2,256]{3,1,2,0:T(4,128)S(1)} %copy.148), channel_id=1, source_target_pairs={{0,1},{1,2},{2,3},{3,4},{4,5},{5,6},{6,7},{7,8},{8,9},{9,10},{10,1... | collective-permute-start | bytes 24584 | tf_op jit(solution)/shard_map/ppermute | solution.py:41
  317.1 7.5 %collective-permute-start.52 = (f32[1,4,2,256]{3,1,2,0:T(4,128)S(1)}, f32[1,4,2,256]{3,1,2,0:T(4,128)S(1)}, u32[]{:S(2)}, u32[]{:S(2)}) collective-permute-start(f32[1,4,2,256]{3,1,2,0:T(4,128)S(1)} %copy.147), channel_id=1, source_target_pairs={{1,0},{2,1},{3,2},{4,3},{5,4},{6,5},{7,6},{8,7},{9,8},{10,9},{11,1... | collective-permute-start | bytes 24584 | tf_op jit(solution)/shard_map/ppermute | solution.py:43
  324.6 115.5 %collective-permute-start.54 = (f32[1,2,8,256]{3,1,2,0:T(2,128)S(1)}, f32[1,2,8,256]{3,1,2,0:T(2,128)S(1)}, u32[]{:S(2)}, u32[]{:S(2)}) collective-permute-start(f32[1,2,8,256]{3,1,2,0:T(2,128)S(1)} %get-tuple-element.110), channel_id=1, source_target_pairs={{32,0},{64,32},{96,64},{128,96},{160,128},{192,160},{224,192},{256... | collective-permute-start | bytes 49160 | tf_op jit(solution)/shard_map/ppermute | solution.py:43
  326.5 113.5 %collective-permute-start.55 = (f32[1,2,8,256]{3,1,2,0:T(2,128)S(1)}, f32[1,2,8,256]{3,1,2,0:T(2,128)S(1)}, u32[]{:S(2)}, u32[]{:S(2)}) collective-permute-start(f32[1,2,8,256]{3,1,2,0:T(2,128)S(1)} %get-tuple-element.109), channel_id=1, source_target_pairs={{0,32},{32,64},{64,96},{96,128},{128,160},{160,192},{192,224},{224... | collective-permute-start | bytes 49160 | tf_op jit(solution)/shard_map/ppermute | solution.py:41
  440.3 9.2 %collective-permute-start.57 = (f32[1,8,2,256]{3,1,2,0:T(8,128)S(1)}, f32[1,8,2,256]{3,1,2,0:T(8,128)S(1)}, u32[]{:S(2)}, u32[]{:S(2)}) collective-permute-start(f32[1,8,2,256]{3,1,2,0:T(8,128)S(1)} %copy.150), channel_id=1, source_target_pairs={{0,1},{1,2},{2,3},{3,4},{4,5},{5,6},{6,7},{7,8},{8,9},{9,10},{10,1... | collective-permute-start | bytes 49160 | tf_op jit(solution)/shard_map/ppermute | solution.py:41
  442.8 7.5 %collective-permute-start.56 = (f32[1,8,2,256]{3,1,2,0:T(8,128)S(1)}, f32[1,8,2,256]{3,1,2,0:T(8,128)S(1)}, u32[]{:S(2)}, u32[]{:S(2)}) collective-permute-start(f32[1,8,2,256]{3,1,2,0:T(8,128)S(1)} %copy.149), channel_id=1, source_target_pairs={{1,0},{2,1},{3,2},{4,3},{5,4},{6,5},{7,6},{8,7},{9,8},{10,9},{11,1... | collective-permute-start | bytes 49160 | tf_op jit(solution)/shard_map/ppermute | solution.py:43
  450.4 160.4 %collective-permute-start.58 = (f32[1,2,16,256]{3,1,2,0:T(2,128)S(1)}, f32[1,2,16,256]{3,1,2,0:T(2,128)S(1)}, u32[]{:S(2)}, u32[]{:S(2)}) collective-permute-start(f32[1,2,16,256]{3,1,2,0:T(2,128)S(1)} %get-tuple-element.78), channel_id=1, source_target_pairs={{32,0},{64,32},{96,64},{128,96},{160,128},{192,160},{224,192},{256... | collective-permute-start | bytes 98312 | tf_op jit(solution)/shard_map/ppermute | solution.py:43
  454.3 156.5 %collective-permute-start.59 = (f32[1,2,16,256]{3,1,2,0:T(2,128)S(1)}, f32[1,2,16,256]{3,1,2,0:T(2,128)S(1)}, u32[]{:S(2)}, u32[]{:S(2)}) collective-permute-start(f32[1,2,16,256]{3,1,2,0:T(2,128)S(1)} %get-tuple-element.77), channel_id=1, source_target_pairs={{0,32},{32,64},{64,96},{96,128},{128,160},{160,192},{192,224},{224... | collective-permute-start | bytes 98312 | tf_op jit(solution)/shard_map/ppermute | solution.py:41
  611.1 9.6 %collective-permute-start.61 = (f32[1,16,2,256]{3,1,2,0:T(8,128)S(1)}, f32[1,16,2,256]{3,1,2,0:T(8,128)S(1)}, u32[]{:S(2)}, u32[]{:S(2)}) collective-permute-start(f32[1,16,2,256]{3,1,2,0:T(8,128)S(1)} %copy.152), channel_id=1, source_target_pairs={{0,1},{1,2},{2,3},{3,4},{4,5},{5,6},{6,7},{7,8},{8,9},{9,10},{10,1... | collective-permute-start | bytes 98312 | tf_op jit(solution)/shard_map/ppermute | solution.py:41
  615.1 6.8 %collective-permute-start.60 = (f32[1,16,2,256]{3,1,2,0:T(8,128)S(1)}, f32[1,16,2,256]{3,1,2,0:T(8,128)S(1)}, u32[]{:S(2)}, u32[]{:S(2)}) collective-permute-start(f32[1,16,2,256]{3,1,2,0:T(8,128)S(1)} %copy.151), channel_id=1, source_target_pairs={{1,0},{2,1},{3,2},{4,3},{5,4},{6,5},{7,6},{8,7},{9,8},{10,9},{11,1... | collective-permute-start | bytes 98312 | tf_op jit(solution)/shard_map/ppermute | solution.py:43
  622.3 6.6 %collective-permute-start.62 = (f32[1,2,32,256]{3,1,2,0:T(2,128)S(1)}, f32[1,2,32,256]{3,1,2,0:T(2,128)S(1)}, u32[]{:S(2)}, u32[]{:S(2)}) collective-permute-start(f32[1,2,32,256]{3,1,2,0:T(2,128)S(1)} %get-tuple-element.50), channel_id=1, source_target_pairs={{32,0},{64,32},{96,64},{128,96},{160,128},{192,160},{224,192},{256... | collective-permute-start | bytes 196616 | tf_op jit(solution)/shard_map/ppermute | solution.py:43
  624.7 4.5 collective-permute-start.63
  (10 other events, 248.2 us)
Sparse Core Ops, SparseCore 0:
  333.2 275.6 all-reduce.1
where the time goes:
time: 641 us; the launch traced here: 638 us
  starting transfers between devices  244 us (38%)
  waiting for transfers between devices  215 us (34%)
  blocking collectives  107 us (17%)
  local copies, waits for them, and re-layouts  35.3 us (6%)
  other arithmetic  17.5 us (3%)
  between operations  16 us (2%)
    psum x1, waiting for transfers between devices, shards(): lax.psum((weight_part, bias_part), ('lat', 'lon'))  153 us
    ppermute x32, starting transfers between devices, with_halo(): lax.ppermute(head, axis, [((i + 1) % count, i) for i in range(ends)])  146 us
    psum x1, blocking collectives, shards(): lax.psum((weight_part, bias_part), ('lat', 'lon'))  107 us
    ppermute x32, starting transfers between devices, with_halo(): lax.ppermute(tail, axis, [(i, (i + 1) % count) for i in range(ends)])  98 us
    ppermute x32, waiting for transfers between devices, with_halo(): lax.ppermute(head, axis, [((i + 1) % count, i) for i in range(ends)])  45.9 us
    slice x56, local copies, waits for them, and re-layouts, reduce_padded(): lax.slice_in_dim(padded, tap_index + 1, tap_index + 1 + count_in, 2, dim_...  27.8 us
    ppermute x32, waiting for transfers between devices, with_halo(): lax.ppermute(tail, axis, [(i, (i + 1) % count) for i in range(ends)])  16.2 us
  transfers between devices with their start and end apart: 65, of which 31 were waited for; matrix products, arithmetic and copies ran while one was open for 1% of the time, Pallas kernels for 0%

commit v1 on v0

v1 whole, which is shorter than its diff:
```python
import functools
import math

import jax
import jax.numpy as jnp
import numpy as np
from jax import lax
from jax.experimental import pallas as pl
from jax.experimental.pallas import tpu as pltpu
from jax.sharding import PartitionSpec as P

MESH = pl.DeviceIdType.MESH
F32 = jnp.float32
BF16 = jnp.bfloat16
ROW = 8

low_taps = (
    -0.010597401784997278,
    0.032883011666982945,
    0.030841381835986965,
    -0.18703481171888114,
    -0.02798376941698385,
    0.6308807679295904,
    0.7148465705525415,
    0.23037781330885523,
)
high_taps = (
    -0.23037781330885523,
    0.7148465705525415,
    -0.6308807679295904,
    -0.02798376941698385,
    0.18703481171888114,
    0.030841381835986965,
    -0.032883011666982945,
    -0.010597401784997278,
)


def level_matrix(count, taps, closed):
    matrix = np.zeros((count // 2, count))
    for k in range(count // 2):
        for j in range(8):
            n = 2 * k + j - 3
            if closed:
                matrix[k, n % count] += taps[j]
            elif 0 <= n < count:
                matrix[k, n] += taps[j]
    return matrix


def analysis_matrix(count, last_taps, closed):
    product = level_matrix(count, low_taps, closed)
    for level in (1, 2):
        product = level_matrix(count >> level, low_taps, closed) @ product
    return level_matrix(count >> 3, last_taps, closed) @ product


def coarse_offset(block, half):
    if block < 3:
        return 2 * (block - 1) + half
    return -3 if half == 1 else 4


def band_tables(nlat, nlon, band, sector):
    lat = analysis_matrix(nlat, low_taps, False)
    lons = [analysis_matrix(nlon, taps, True) for taps in (low_taps, high_taps)]
    bands = nlat // band
    tables = []
    for d in (0, bands // 2, bands - 1):
        rows = np.zeros((4, 2, band))
        for block in range(4):
            for p in range(2):
                k = 2 * d + coarse_offset(block, p)
                if 0 <= k < lat.shape[0]:
                    rows[block, p] = lat[k, d * band : (d + 1) * band]
        cols = np.zeros((4, 2, 2, sector))
        for block in range(4):
            for q in range(2):
                k = (2 + coarse_offset(block, q)) % lons[0].shape[0]
                for f in range(2):
                    cols[block, q, f] = lons[f][k, sector : 2 * sector]
        table = np.einsum("apn,bqfm->abpqfnm", rows, cols)
        tables.append(table.reshape(128, band * sector))
    full = np.stack(tables).astype(np.float32)
    high = full.astype(jnp.bfloat16)
    low = (full - high.astype(np.float32)).astype(jnp.bfloat16)
    return np.concatenate([high, low], axis=1)


def kernel(
    dims, x_hbm, cot_hbm, mixl_hbm, mixh_hbm, w_hbm, bias_hbm, k_hbm,
    fg_hbm, mlg_hbm, mhg_hbm, wg_hbm, bg_hbm,
    x_v, cot_v, mixl_v, mixh_v, w_v, bias_v, kd_v,
    ku_v, xt_v, wt_v, ghi_v, glo_v, mm_v, ml_v, bacc_v,
    fg_v, mlg_v, mhg_v, wg_v, bg_v,
    as_v, ar_v, ss_v, sr_v, gm_v, gr_v, gs_v, gg_v,
    cs_v, cr_v, xs_v, xr_v, zs_v, zr_v, ys_v, yr_v, af_v,
    in_sem, out_sem, h_send, h_recv, r_send, r_recv,
):
    nlat, nlon, ncells = dims
    nz, ny = nlat // 2, min(ROW, nlon // 2)
    nx = nlon // ny
    tx = 32 // nx
    tz = tx // nz
    lat, lon = lax.axis_index("lat"), lax.axis_index("lon")
    core, z = lax.rem(lat, 2), lat // 2
    y, x = lax.rem(lon, ny), lon // ny

    def at_lat(step):
        return {"lat": lax.rem(lat + step + nlat, nlat)}

    def at_lon(step):
        return {"lon": lax.rem(lon + step + nlon, nlon)}

    partner = {"lat": lat + 1 - 2 * core}

    def at_z(k):
        return lax.rem(z + k, nz)

    def at_x(k):
        return lax.rem(x + k, nx)

    def at_y(k):
        return lax.rem(y + k, ny)

    variant = (lat + nlat - 2) // (nlat - 1) + lat // (nlat - 1)
    loads = [
        (x_hbm, x_v), (k_hbm.at[variant], kd_v), (w_hbm, w_v), (bias_hbm, bias_v),
        (mixl_hbm, mixl_v), (mixh_hbm, mixh_v), (cot_hbm, cot_v),
    ]
    loads = [pltpu.make_async_copy(s, d, in_sem.at[i]) for i, (s, d) in enumerate(loads)]
    for copy in loads:
        copy.start()

    barrier = pltpu.get_barrier_semaphore()
    near = [at_lat(1), at_lat(-1), at_lon(1), at_lon(-1), at_lon(2), at_lon(-2)]
    near += [{"lat": at_z(k) * 2 + core} for k in range(1, nz)]
    near += [{"lon": at_x(k) * ny + y} for k in range(1, nx)]
    near += [{"lon": x * ny + at_y(k)} for k in range(1, ny)]
    for device in near:
        pl.semaphore_signal(barrier, inc=1, device_id=device, device_id_type=MESH)

    sends = []

    def push(src, dst, send_sem, recv_sem, device):
        copy = pltpu.make_async_remote_copy(
            src_ref=src, dst_ref=dst, send_sem=send_sem, recv_sem=recv_sem,
            device_id=device, device_id_type=MESH,
        )
        copy.start()
        sends.append(copy)
        return copy

    row = lax.broadcasted_iota(jnp.int32, (8, 256), 0)
    lower_p = row < 4
    lower_q = lax.rem(row // 2, 2) < 1
    below = jnp.where(lat >= 2, 1.0, 0.0)
    above = jnp.where(lat + 2 < nlat, 1.0, 0.0)

    def partial_lat_start(e, hi, lo):
        if lo is None:
            whole = jnp.dot(kd_v[...], hi, preferred_element_type=F32)
            part = whole[:128] + whole[128:]
        else:
            whole = jnp.dot(kd_v[...], hi, preferred_element_type=F32)
            part = whole[:128] + whole[128:]
            part = part + jnp.dot(kd_v[:128], lo, preferred_element_type=F32)
        as_v[e] = part.reshape(4, 4, 8, 256)

    def partial_lat_send(e):
        plan = ((0, 0, -1), (2, 1, 1), (3, 2, -2), (3, 3, 2))
        return [
            push(as_v.at[e, block], ar_v.at[e, slot], h_send.at[e, 0, slot],
                 h_recv.at[e, 0, slot], at_lat(step))
            for block, slot, step in plan
        ]

    def partial_lon(e, copies):
        for copy in copies:
            copy.wait_recv()
        for tile in range(4):
            far = jnp.where(lower_p, ar_v[e, 3, tile] * below, ar_v[e, 2, tile] * above)
            ss_v[e, tile] = (as_v[e, 1, tile] + ar_v[e, 0, tile]) + (ar_v[e, 1, tile] + far)
        plan = ((0, 0, -1), (2, 1, 1), (3, 2, -2), (3, 3, 2))
        return [
            push(ss_v.at[e, tile], sr_v.at[e, slot], h_send.at[e, 1, slot],
                 h_recv.at[e, 1, slot], at_lon(step))
            for tile, slot, step in plan
        ]

    def partial_done(e, copies):
        for copy in copies:
            copy.wait_recv()
        far = jnp.where(lower_q, sr_v[e, 3], sr_v[e, 2])
        return (ss_v[e, 1] + sr_v[e, 0]) + (sr_v[e, 1] + far)

    def spread_lon(e, tile):
        gm_v[e] = tile
        plan = ((0, 1), (1, -1), (2, 2), (3, -2))
        return [
            push(gm_v.at[e], gr_v.at[e, slot], h_send.at[e, 2, slot],
                 h_recv.at[e, 2, slot], at_lon(step))
            for slot, step in plan
        ]

    def spread_lat(e, copies):
        for copy in copies:
            copy.wait_recv()
        gs_v[e, 0] = gr_v[e, 0]
        gs_v[e, 1] = gm_v[e]
        gs_v[e, 2] = gr_v[e, 1]
        gs_v[e, 3] = jnp.where(lower_q, gr_v[e, 3], gr_v[e, 2])
        plan = ((0, 1), (1, -1), (2, 2), (3, -2))
        return [
            push(gs_v.at[e], gg_v.at[e, slot], h_send.at[e, 3, slot],
                 h_recv.at[e, 3, slot], at_lat(step))
            for slot, step in plan
        ]

    def spread_done(e, copies):
        for copy in copies:
            copy.wait_recv()
        far = jnp.where(lower_p[None], gg_v[e, 3] * above, gg_v[e, 2] * below)
        parts = (gg_v[e, 0], gs_v[e], gg_v[e, 1], far)
        for block, part in enumerate(parts):
            part = part.reshape(32, 256)
            high = part.astype(BF16)
            low = (part - high.astype(F32)).astype(BF16)
            mm_v[pl.ds(32 * block, 32), :] = high
            mm_v[pl.ds(128 + 32 * block, 32), :] = high
            ml_v[pl.ds(32 * block, 32), :] = low

    def picked(tile, r):
        return jnp.where(row == r, tile, 0.0).astype(BF16)

    def mixer(r):
        p, q, f = r // 4, (r // 2) % 2, r % 2
        return (mixh_v if f else mixl_v)[p, q]

    loads[0].wait()
    loads[1].wait()
    partial_lat_start(0, x_v[...], None)
    pl.semaphore_wait(barrier, len(near))
    copies = partial_lat_send(0)

    loads[2].wait()
    loads[3].wait()
    ku_v[...] = kd_v[...].T
    xt_v[...] = x_v[...].T
    wt_v[...] = w_v[...].T
    loads[4].wait()
    loads[5].wait()
    loads[6].wait()

    copies = partial_lon(0, copies)
    coarse = partial_done(0, copies).astype(BF16).astype(F32)
    mixed = jnp.dot(picked(coarse, 0), mixer(0), preferred_element_type=F32)
    for r in range(1, 8):
        mixed = mixed + jnp.dot(picked(coarse, r), mixer(r), preferred_element_type=F32)
    copies = spread_lon(0, mixed)
    copies = spread_lat(0, copies)
    spread_done(0, copies)

    bacc_v[...] = jnp.zeros_like(bacc_v)
    chunk = 256

    def gate(i, carry):
        rows = pl.ds(pl.multiple_of(i * chunk, chunk), chunk)
        pre = jnp.dot(ku_v[rows, :], mm_v[...], preferred_element_type=F32)
        pre = pre + jnp.dot(ku_v[rows, :128], ml_v[...], preferred_element_type=F32)
        pre = pre + jnp.dot(x_v[rows, :], w_v[...], preferred_element_type=F32)
        pre = pre + bias_v[...]
        cdf = 0.5 * (1.0 + lax.erf(pre * (1.0 / math.sqrt(2.0))))
        pdf = jnp.exp(-0.5 * pre * pre) * (1.0 / math.sqrt(2.0 * math.pi))
        grad = cot_v[rows, :].astype(F32) * (cdf + pre * pdf)
        high = grad.astype(BF16)
        ghi_v[rows, :] = high
        glo_v[rows, :] = (grad - high.astype(F32)).astype(BF16)
        bacc_v[...] += jnp.sum(grad.reshape(chunk // 8, 8, 256), axis=0)
        return carry

    lax.fori_loop(0, 1024 // chunk, gate, 0)

    total = jnp.dot(xt_v[...], ghi_v[...], preferred_element_type=F32)
    bias_sum = jnp.sum(bacc_v[...], axis=0, keepdims=True)
    row1 = lax.broadcasted_iota(jnp.int32, (8, 128), 0)
    bias_tile = jnp.where(row1 == 0, bias_sum[:, :128], 0.0)
    bias_tile = jnp.where(row1 == 1, bias_sum[:, 128:], bias_tile)
    for h in range(2):
        cs_v[h, :32] = total[:, h * 128 : (h + 1) * 128].reshape(32, 8, 128)
        cs_v[h, 32] = bias_tile
    sem = iter(range(64))
    k = next(sem)
    core_copy = push(cs_v.at[1 - core], cr_v, r_send.at[k], r_recv.at[k], partner)

    partial_lat_start(1, ghi_v[...], glo_v[...])
    copies = partial_lat_send(1)

    core_copy.wait_recv()
    red = cs_v[core, :32] + cr_v[:32]
    red_bias = cs_v[core, 32] + cr_v[32]
    for j in range(nx):
        xs_v[j, :tx] = red[j * tx : (j + 1) * tx]
        xs_v[j, tx] = red_bias
    xr_v[x] = xs_v[x]
    x_copies = []
    for j in range(1, nx):
        k = next(sem)
        x_copies.append(push(xs_v.at[at_x(j)], xr_v.at[x], r_send.at[k], r_recv.at[k],
                             {"lon": at_x(j) * ny + y}))

    copies = partial_lon(1, copies)

    for copy in x_copies:
        copy.wait_recv()
    red = xr_v[0]
    for j in range(1, nx):
        red = red + xr_v[j]
    for j in range(nz):
        zs_v[j, :tz] = red[j * tz : (j + 1) * tz]
        zs_v[j, tz] = red[tx]
    zr_v[z] = zs_v[z]
    z_copies = []
    for j in range(1, nz):
        k = next(sem)
        z_copies.append(push(zs_v.at[at_z(j)], zr_v.at[z], r_send.at[k], r_recv.at[k],
                             {"lat": at_z(j) * 2 + core}))

    back = partial_done(1, copies)
    back_rounded = back.astype(BF16).astype(F32)
    pull = None
    for r in range(8):
        term = lax.dot_general(picked(back_rounded, r), mixer(r), (((1,), (1,)), ((), ())),
                               preferred_element_type=F32)
        pull = term if pull is None else pull + term
    copies = spread_lon(1, pull)

    for copy in z_copies:
        copy.wait_recv()
    red = zr_v[0]
    for j in range(1, nz):
        red = red + zr_v[j]
    ys_v[...] = red
    yr_v[y] = red
    y_copies = []
    for j in range(1, ny):
        k = next(sem)
        y_copies.append(push(ys_v, yr_v.at[y], r_send.at[k], r_recv.at[k],
                             {"lon": x * ny + at_y(j)}))

    copies = spread_lat(1, copies)

    columns = coarse.T
    for r in range(8):
        p, q, f = r // 4, (r // 2) % 2, r % 2
        outer = (columns[:, r : r + 1] * back[r : r + 1, :]).astype(BF16)
        (mhg_v if f else mlg_v)[p, q] = outer
    outs = [pltpu.make_async_copy(mlg_v, mlg_hbm, out_sem.at[0]),
            pltpu.make_async_copy(mhg_v, mhg_hbm, out_sem.at[1])]
    for copy in outs:
        copy.start()

    for copy in y_copies:
        copy.wait_recv()
    red = yr_v[0]
    for j in range(1, ny):
        red = red + yr_v[j]
    red = red * (1.0 / math.sqrt(ncells))
    af_v[core, x, z] = red[:tz]
    z_copies = []
    for j in range(1, nz):
        k = next(sem)
        z_copies.append(push(af_v.at[core, x, z], af_v.at[core, x, z], r_send.at[k], r_recv.at[k],
                             {"lat": at_z(j) * 2 + core}))
    bg_v[:, :128] = red[tz][0:1, :]
    bg_v[:, 128:] = red[tz][1:2, :]

    spread_done(1, copies)

    def back_out(i, carry):
        rows = pl.ds(pl.multiple_of(i * chunk, chunk), chunk)
        out = jnp.dot(ku_v[rows, :], mm_v[...], preferred_element_type=F32)
        out = out + jnp.dot(ku_v[rows, :128], ml_v[...], preferred_element_type=F32)
        out = out + jnp.dot(ghi_v[rows, :], wt_v[...], preferred_element_type=F32)
        fg_v[rows, :] = out.astype(BF16)
        return carry

    lax.fori_loop(0, 1024 // chunk, back_out, 0)
    outs.append(pltpu.make_async_copy(fg_v, fg_hbm, out_sem.at[2]))
    outs[-1].start()

    for copy in z_copies:
        copy.wait_recv()
    x_copies = []
    for j in range(1, nx):
        k = next(sem)
        x_copies.append(push(af_v.at[core, x], af_v.at[core, x], r_send.at[k], r_recv.at[k],
                             {"lon": at_x(j) * ny + y}))
    for copy in x_copies:
        copy.wait_recv()
    k = next(sem)
    core_copy = push(af_v.at[core], af_v.at[core], r_send.at[k], r_recv.at[k], partner)
    core_copy.wait_recv()
    for h in range(2):
        wg_v[:, h * 128 : (h + 1) * 128] = af_v[h].reshape(256, 128)
    outs.append(pltpu.make_async_copy(wg_v, wg_hbm, out_sem.at[3]))
    outs.append(pltpu.make_async_copy(bg_v, bg_hbm, out_sem.at[4]))
    for copy in outs[3:]:
        copy.start()
    for copy in outs:
        copy.wait()
    for copy in sends:
        copy.wait_send()


def shards(fields, cotangent, mix_low, mix_high, point_weight, point_bias):
    nlat, nlon = lax.axis_size("lat"), lax.axis_size("lon")
    rows, cols, channels = fields.shape
    cells = rows * cols
    tables = jnp.asarray(band_tables(rows * nlat, cols * nlon, rows, cols))
    nz, ny = nlat // 2, min(ROW, nlon // 2)
    nx = nlon // ny
    tx = 32 // nx
    tz = tx // nz
    messages = 2 + 2 * (nx - 1) + 2 * (nz - 1) + (ny - 1)
    vmem = pltpu.VMEM
    scratch = [
        vmem((cells, channels), BF16), vmem((cells, channels), BF16),
        vmem(mix_low.shape, BF16), vmem(mix_high.shape, BF16),
        vmem((channels, channels), BF16), vmem((1, channels), F32), vmem((256, cells), BF16),
        vmem((cells, 256), BF16), vmem((channels, cells), BF16), vmem((channels, channels), BF16),
        vmem((cells, channels), BF16), vmem((cells, channels), BF16),
        vmem((256, channels), BF16), vmem((128, channels), BF16), vmem((8, channels), F32),
        vmem((cells, channels), BF16), vmem(mix_low.shape, BF16), vmem(mix_high.shape, BF16),
        vmem((channels, channels), F32), vmem((1, channels), F32),
        vmem((2, 4, 4, 8, channels), F32), vmem((2, 4, 4, 8, channels), F32),
        vmem((2, 4, 8, channels), F32), vmem((2, 4, 8, channels), F32),
        vmem((2, 8, channels), F32), vmem((2, 4, 8, channels), F32),
        vmem((2, 4, 8, channels), F32), vmem((2, 4, 4, 8, channels), F32),
        vmem((2, 33, 8, 128), F32), vmem((33, 8, 128), F32),
        vmem((nx, tx + 1, 8, 128), F32), vmem((nx, tx + 1, 8, 128), F32),
        vmem((nz, tz + 1, 8, 128), F32), vmem((nz, tz + 1, 8, 128), F32),
        vmem((tz + 1, 8, 128), F32), vmem((ny, tz + 1, 8, 128), F32),
        vmem((2, nx, nz, tz, 8, 128), F32),
        pltpu.SemaphoreType.DMA((7,)), pltpu.SemaphoreType.DMA((5,)),
        pltpu.SemaphoreType.DMA((2, 4, 4)), pltpu.SemaphoreType.DMA((2, 4, 4)),
        pltpu.SemaphoreType.DMA((messages,)), pltpu.SemaphoreType.DMA((messages,)),
    ]
    outs = pl.pallas_call(
        functools.partial(kernel, (nlat, nlon, cells * nlat * nlon)),
        out_shape=(
            jax.ShapeDtypeStruct((cells, channels), BF16),
            jax.ShapeDtypeStruct(mix_low.shape, BF16),
            jax.ShapeDtypeStruct(mix_high.shape, BF16),
            jax.ShapeDtypeStruct((channels, channels), F32),
            jax.ShapeDtypeStruct((1, channels), F32),
        ),
        in_specs=[pl.BlockSpec(memory_space=pl.ANY)] * 7,
        out_specs=[pl.BlockSpec(memory_space=pl.ANY)] * 5,
        scratch_shapes=scratch,
        compiler_params=pltpu.CompilerParams(
            collective_id=0, has_side_effects=True, vmem_limit_bytes=32 * 1024 * 1024
        ),
        name="wavelet_block",
    )(
        fields.reshape(cells, channels), cotangent.reshape(cells, channels), mix_low, mix_high,
        point_weight, point_bias.reshape(1, channels), tables,
    )
    return (
        outs[0].reshape(fields.shape), outs[1], outs[2], outs[3], outs[4].reshape(channels),
    )


def solution(mesh):
    placed = (
        P("lat", "lon", None),
        P("lat", "lon", None),
        P("lat", "lon", None, None),
        P("lat", "lon", None, None),
        P(),
        P(),
    )
    return jax.shard_map(
        shards,
        mesh=mesh,
        in_specs=placed,
        out_specs=(
            P("lat", "lon", None),
            P("lat", "lon", None, None),
            P("lat", "lon", None, None),
            P(),
            P(),
        ),
        check_vma=False,
    )
```

time: 641 us -> 71.4 us (0.11)
  starting transfers between devices: 244 us -> 0 us
  waiting for transfers between devices: 215 us -> 0 us
  blocking collectives: 107 us -> 0 us
  Pallas kernels: 0 us -> 59.6 us
  local copies, waits for them, and re-layouts: 35.3 us -> 10.8 us
  other arithmetic: 17.5 us -> 0 us
  between operations: 16 us -> 0.66 us
    ppermute x64 -> x0, starting transfers between devices: 244 us -> none  [the longest x32 146 us: with_halo(): lax.ppermute(head, axis, [((i + 1) % count, i) for i in range(ends)])]
    psum x1 -> x0, waiting for transfers between devices: 153 us -> none  [shards(): lax.psum((weight_part, bias_part), ('lat', 'lon'))]
    psum x1 -> x0, blocking collectives: 107 us -> none  [shards(): lax.psum((weight_part, bias_part), ('lat', 'lon'))]
    ppermute x64 -> x0, waiting for transfers between devices: 62.1 us -> none  [the longest x32 45.9 us: with_halo(): lax.ppermute(head, axis, [((i + 1) % count, i) for i in range(ends)])]
    pallas_call x0 -> x1, Pallas kernels: none -> 59.6 us  [shards(): pl.pallas_call(functools.partial(kernel, (nlat, nlon, cells * nlat * nlon...]
    slice x88 -> x0, local copies, waits for them, and re-layouts: 31.2 us -> none  [the longest x56 27.8 us: reduce_padded(): lax.slice_in_dim(padded, tap_index + 1, tap_index + 1 + count_in, 2, dim_...]
    unnamed x37 -> x19, local copies, waits for them, and re-layouts: 2.01 us -> 10.8 us
  transfers between devices with their start and end apart: 65 -> 0, of which waited for: 31 -> 0; matrix products, arithmetic and copies ran while one was open for 1% -> 0% of each run, Pallas kernels for 0% -> 0%
where the time goes in v1:
time: 71.4 us; the launch traced here: 71 us
  Pallas kernels  59.6 us (83%)
  local copies, waits for them, and re-layouts  10.8 us (15%)
    pallas_call x1, Pallas kernels, shards(): pl.pallas_call(functools.partial(kernel, (nlat, nlon, cells * nlat * nlon...  59.6 us
    unnamed x19, local copies, waits for them, and re-layouts  10.8 us

profile of v1, /device:TPU:1, one launch (start us, length us, event | category | flops | bytes accessed | tf_op | source)
XLA Modules:
  0.0 71.0 jit_solution(2816014130770961998)
XLA Ops:
  0.6 0.0 copy-start
  0.6 1.4 %copy-done = bf16[3,256,1024]{2,1,0:T(8,128)(2,1)S(1)} copy-done((bf16[3,256,1024]{2,1,0:T(8,128)(2,1)S(1)}, bf16[3,256,1024]{2,1,0:T(8,128)(2,1)}, u32[]{:S(2)}) %copy-start) | copy-done | bytes 1572888
  2.0 0.0 copy-start.1
  2.0 1.0 %copy-done.1 = bf16[32,32,256]{2,1,0:T(8,128)(2,1)S(1)} copy-done((bf16[32,32,256]{2,1,0:T(8,128)(2,1)S(1)}, bf16[32,32,256]{2,1,0:T(8,128)(2,1)}, u32[]{:S(2)}) %copy-start.1) | copy-done | bytes 524312
  3.1 0.0 copy-start.2
  3.1 1.0 %copy-done.2 = bf16[32,32,256]{2,1,0:T(8,128)(2,1)S(1)} copy-done((bf16[32,32,256]{2,1,0:T(8,128)(2,1)S(1)}, bf16[32,32,256]{2,1,0:T(8,128)(2,1)}, u32[]{:S(2)}) %copy-start.2) | copy-done | bytes 524312
  4.1 0.0 copy-start.3
  4.1 1.0 %copy-done.3 = bf16[2,2,256,256]{3,2,1,0:T(8,128)(2,1)S(1)} copy-done((bf16[2,2,256,256]{3,2,1,0:T(8,128)(2,1)S(1)}, bf16[2,2,256,256]{3,2,1,0:T(8,128)(2,1)}, u32[]{:S(2)}) %copy-start.3) | copy-done | bytes 524312
  5.2 0.0 copy-start.4
  5.2 1.0 %copy-done.4 = bf16[2,2,256,256]{3,2,1,0:T(8,128)(2,1)S(1)} copy-done((bf16[2,2,256,256]{3,2,1,0:T(8,128)(2,1)S(1)}, bf16[2,2,256,256]{3,2,1,0:T(8,128)(2,1)}, u32[]{:S(2)}) %copy-start.4) | copy-done | bytes 524312
  6.2 0.0 copy-start.5
  6.2 0.9 %copy-done.5 = bf16[256,256]{1,0:T(8,128)(2,1)S(1)} copy-done((bf16[256,256]{1,0:T(8,128)(2,1)S(1)}, bf16[256,256]{1,0:T(8,128)(2,1)}, u32[]{:S(2)}) %copy-start.5) | copy-done | bytes 131096
  7.1 0.0 copy-start.6
  7.1 0.7 copy-done.6
  7.8 59.6 %wavelet_block.1 = (bf16[1024,256]{1,0:T(8,128)(2,1)S(1)}, bf16[2,2,256,256]{3,2,1,0:T(8,128)(2,1)S(1)}, bf16[2,2,256,256]{3,2,1,0:T(8,128)(2,1)S(1)}, f32[256,256]{1,0:T(8,128)S(1)}, f32[1,256]{1,0:T(1,128)S(1)}) custom-call(bf16[1024,256]{1,0:T(8,128)(2,1)S(1)} %bitcast.6, bf16[1024,256]{1,0:T(8,128)(2,1)S(1)} %bitcast.7, ...), custom_call_target="tpu_custom_call" | custom-call | tf_op jit(solution)/shard_map/wavelet_block/pallas_call | solution.py:449
  67.4 0.8 %copy.17 = bf16[32,32,256]{2,1,0:T(8,128)(2,1)} copy(bf16[32,32,256]{2,1,0:T(8,128)(2,1)S(1)} %bitcast.5) | data formatting | bytes 1048576
  68.2 0.8 %copy.18 = bf16[2,2,256,256]{3,2,1,0:T(8,128)(2,1)} copy(bf16[2,2,256,256]{3,2,1,0:T(8,128)(2,1)S(1)} %get-tuple-element.21) | data formatting | bytes 1048576
  69.0 0.8 %copy.19 = bf16[2,2,256,256]{3,2,1,0:T(8,128)(2,1)} copy(bf16[2,2,256,256]{3,2,1,0:T(8,128)(2,1)S(1)} %get-tuple-element.22) | data formatting | bytes 1048576
  69.8 0.7 copy.20
  70.5 0.6 copy.21
Async XLA Ops:
  0.6 1.4 %copy-start = (bf16[3,256,1024]{2,1,0:T(8,128)(2,1)S(1)}, bf16[3,256,1024]{2,1,0:T(8,128)(2,1)}, u32[]{:S(2)}) copy-start(bf16[3,256,1024]{2,1,0:T(8,128)(2,1)} %constant.2.clone.k_hbm) | copy-start | bytes 4718596
  2.0 1.0 %copy-start.1 = (bf16[32,32,256]{2,1,0:T(8,128)(2,1)S(1)}, bf16[32,32,256]{2,1,0:T(8,128)(2,1)}, u32[]{:S(2)}) copy-start(bf16[32,32,256]{2,1,0:T(8,128)(2,1)} %param.7) | copy-start | bytes 1572868
  3.1 1.0 %copy-start.2 = (bf16[32,32,256]{2,1,0:T(8,128)(2,1)S(1)}, bf16[32,32,256]{2,1,0:T(8,128)(2,1)}, u32[]{:S(2)}) copy-start(bf16[32,32,256]{2,1,0:T(8,128)(2,1)} %param.8) | copy-start | bytes 1572868
  4.1 1.0 %copy-start.3 = (bf16[2,2,256,256]{3,2,1,0:T(8,128)(2,1)S(1)}, bf16[2,2,256,256]{3,2,1,0:T(8,128)(2,1)}, u32[]{:S(2)}) copy-start(bf16[2,2,256,256]{3,2,1,0:T(8,128)(2,1)} %mixl_hbm.1) | copy-start | bytes 1572868
  5.2 1.0 %copy-start.4 = (bf16[2,2,256,256]{3,2,1,0:T(8,128)(2,1)S(1)}, bf16[2,2,256,256]{3,2,1,0:T(8,128)(2,1)}, u32[]{:S(2)}) copy-start(bf16[2,2,256,256]{3,2,1,0:T(8,128)(2,1)} %mixh_hbm.1) | copy-start | bytes 1572868
  6.2 0.9 %copy-start.5 = (bf16[256,256]{1,0:T(8,128)(2,1)S(1)}, bf16[256,256]{1,0:T(8,128)(2,1)}, u32[]{:S(2)}) copy-start(bf16[256,256]{1,0:T(8,128)(2,1)} %w_hbm.1) | copy-start | bytes 393220
  7.1 0.7 copy-start.6

commit v2 on v1

--- a/solution.py
+++ b/solution.py
@@ -89,13 +89,13 @@
 
 def kernel(
     dims, x_hbm, cot_hbm, mixl_hbm, mixh_hbm, w_hbm, bias_hbm, k_hbm,
-    fg_hbm, mlg_hbm, mhg_hbm, wg_hbm, bg_hbm,
+    fg_v, mlg_v, mhg_v, af_v, bg_v,
     x_v, cot_v, mixl_v, mixh_v, w_v, bias_v, kd_v,
     ku_v, xt_v, wt_v, ghi_v, glo_v, mm_v, ml_v, bacc_v,
-    fg_v, mlg_v, mhg_v, wg_v, bg_v,
     as_v, ar_v, ss_v, sr_v, gm_v, gr_v, gs_v, gg_v,
-    cs_v, cr_v, xs_v, xr_v, zs_v, zr_v, ys_v, yr_v, af_v,
-    in_sem, out_sem, h_send, h_recv, r_send, r_recv,
+    cs_v, cr_v, xs_v, xr_v, zs_v, zr_v, ys_v, yr_v,
+    bs_v, bc_v, br_v,
+    in_sem, h_send, h_recv, r_send, r_recv,
 ):
     nlat, nlon, ncells = dims
     nz, ny = nlat // 2, min(ROW, nlon // 2)
@@ -282,49 +282,81 @@
     lax.fori_loop(0, 1024 // chunk, gate, 0)
 
     total = jnp.dot(xt_v[...], ghi_v[...], preferred_element_type=F32)
+    for h in range(2):
+        cs_v[h] = total[:, h * 128 : (h + 1) * 128].reshape(32, 8, 128)
+    sem = iter(range(r_send.shape[0]))
+
+    def send(src, dst, device):
+        k = next(sem)
+        return push(src, dst, r_send.at[k], r_recv.at[k], device)
+
+    core_copy = send(cs_v.at[1 - core], cr_v, partner)
     bias_sum = jnp.sum(bacc_v[...], axis=0, keepdims=True)
-    row1 = lax.broadcasted_iota(jnp.int32, (8, 128), 0)
-    bias_tile = jnp.where(row1 == 0, bias_sum[:, :128], 0.0)
-    bias_tile = jnp.where(row1 == 1, bias_sum[:, 128:], bias_tile)
-    for h in range(2):
-        cs_v[h, :32] = total[:, h * 128 : (h + 1) * 128].reshape(32, 8, 128)
-        cs_v[h, 32] = bias_tile
-    sem = iter(range(64))
-    k = next(sem)
-    core_copy = push(cs_v.at[1 - core], cr_v, r_send.at[k], r_recv.at[k], partner)
+    bs_v[0, 0:1] = bias_sum[:, :128]
+    bs_v[0, 1:2] = bias_sum[:, 128:]
+    bias_core = send(bs_v.at[0], bc_v, partner)
 
     partial_lat_start(1, ghi_v[...], glo_v[...])
     copies = partial_lat_send(1)
 
+    z_order = sorted(range(nz), key=lambda k: -min(k, nz - k))
+    x_order = sorted(range(1, nx), key=lambda k: -min(k, nx - k))
+    y_order = sorted(range(1, ny), key=lambda k: -min(k, ny - k))
+    cuts = sorted({0, 1, 3, 5, nz})
+    groups = [(i, j) for i, j in zip(cuts, cuts[1:]) if j <= nz]
+    if nz < 8:
+        groups = [(i, i + 1) for i in range(nz)]
+
     core_copy.wait_recv()
-    red = cs_v[core, :32] + cr_v[:32]
-    red_bias = cs_v[core, 32] + cr_v[32]
-    for j in range(nx):
-        xs_v[j, :tx] = red[j * tx : (j + 1) * tx]
-        xs_v[j, tx] = red_bias
-    xr_v[x] = xs_v[x]
     x_copies = []
-    for j in range(1, nx):
-        k = next(sem)
-        x_copies.append(push(xs_v.at[at_x(j)], xr_v.at[x], r_send.at[k], r_recv.at[k],
-                             {"lon": at_x(j) * ny + y}))
+    for start, stop in groups:
+        waits = []
+        for i in range(start, stop):
+            part = pl.ds((x * nz + at_z(z_order[i])) * tz, tz)
+            xr_v[x, i] = cs_v[core, part] + cr_v[part]
+        for d, k in enumerate(x_order):
+            for i in range(start, stop):
+                part = pl.ds((at_x(k) * nz + at_z(z_order[i])) * tz, tz)
+                xs_v[d, i] = cs_v[core, part] + cr_v[part]
+            span = pl.ds(start, stop - start)
+            waits.append(send(xs_v.at[d, span], xr_v.at[x, span], {"lon": at_x(k) * ny + y}))
+        x_copies.append(waits)
+
+    def bias_spread(i, order, slot, device):
+        bs_v[i] = bias_part
+        br_v[i, slot] = bias_part
+        return [send(bs_v.at[i], br_v.at[i, slot], device(k)) for k in order]
+
+    def bias_add(i, count, waits):
+        for copy in waits:
+            copy.wait_recv()
+        whole = br_v[i, 0]
+        for j in range(1, count):
+            whole = whole + br_v[i, j]
+        return whole
+
+    bias_core.wait_recv()
+    bias_part = bs_v[0] + bc_v[...]
+    bias_waits = bias_spread(1, x_order, x, lambda k: {"lon": at_x(k) * ny + y})
 
     copies = partial_lon(1, copies)
 
-    for copy in x_copies:
-        copy.wait_recv()
-    red = xr_v[0]
-    for j in range(1, nx):
-        red = red + xr_v[j]
-    for j in range(nz):
-        zs_v[j, :tz] = red[j * tz : (j + 1) * tz]
-        zs_v[j, tz] = red[tx]
-    zr_v[z] = zs_v[z]
     z_copies = []
-    for j in range(1, nz):
-        k = next(sem)
-        z_copies.append(push(zs_v.at[at_z(j)], zr_v.at[z], r_send.at[k], r_recv.at[k],
-                             {"lat": at_z(j) * 2 + core}))
+    for (start, stop), waits in zip(groups, x_copies):
+        for copy in waits:
+            copy.wait_recv()
+        for i in range(start, stop):
+            k = z_order[i]
+            part = xr_v[0, i]
+            for j in range(1, nx):
+                part = part + xr_v[j, i]
+            if k == 0:
+                zr_v[z] = part
+            else:
+                zs_v[i] = part
+                z_copies.append(send(zs_v.at[i], zr_v.at[z], {"lat": at_z(k) * 2 + core}))
+    bias_part = bias_add(1, nx, bias_waits)
+    bias_waits = bias_spread(2, z_order[:-1], z, lambda k: {"lat": at_z(k) * 2 + core})
 
     back = partial_done(1, copies)
     back_rounded = back.astype(BF16).astype(F32)
@@ -342,11 +374,9 @@
         red = red + zr_v[j]
     ys_v[...] = red
     yr_v[y] = red
-    y_copies = []
-    for j in range(1, ny):
-        k = next(sem)
-        y_copies.append(push(ys_v, yr_v.at[y], r_send.at[k], r_recv.at[k],
-                             {"lon": x * ny + at_y(j)}))
+    y_copies = [send(ys_v, yr_v.at[y], {"lon": x * ny + at_y(k)}) for k in y_order]
+    bias_part = bias_add(2, nz, bias_waits)
+    bias_waits = bias_spread(3, y_order, y, lambda k: {"lon": x * ny + at_y(k)})
 
     copies = spread_lat(1, copies)
 
@@ -355,25 +385,23 @@
         p, q, f = r // 4, (r // 2) % 2, r % 2
         outer = (columns[:, r : r + 1] * back[r : r + 1, :]).astype(BF16)
         (mhg_v if f else mlg_v)[p, q] = outer
-    outs = [pltpu.make_async_copy(mlg_v, mlg_hbm, out_sem.at[0]),
-            pltpu.make_async_copy(mhg_v, mhg_hbm, out_sem.at[1])]
-    for copy in outs:
-        copy.start()
 
     for copy in y_copies:
         copy.wait_recv()
     red = yr_v[0]
     for j in range(1, ny):
         red = red + yr_v[j]
-    red = red * (1.0 / math.sqrt(ncells))
-    af_v[core, x, z] = red[:tz]
-    z_copies = []
-    for j in range(1, nz):
-        k = next(sem)
-        z_copies.append(push(af_v.at[core, x, z], af_v.at[core, x, z], r_send.at[k], r_recv.at[k],
-                             {"lat": at_z(j) * 2 + core}))
-    bg_v[:, :128] = red[tz][0:1, :]
-    bg_v[:, 128:] = red[tz][1:2, :]
+    af_v[core, x, z] = red * (1.0 / math.sqrt(ncells))
+
+    def own(k):
+        return af_v.at[core, x, lax.rem(z - k + nz, nz)]
+
+    z_copies = {}
+    for k in z_order[:-1]:
+        z_copies[k] = send(own(0), own(0), {"lat": at_z(k) * 2 + core})
+    x_copies = {k: [] for k in x_order}
+    for k in x_order:
+        x_copies[k].append(send(own(0), own(0), {"lon": at_x(k) * ny + y}))
 
     spread_done(1, copies)
 
@@ -386,31 +414,42 @@
         return carry
 
     lax.fori_loop(0, 1024 // chunk, back_out, 0)
-    outs.append(pltpu.make_async_copy(fg_v, fg_hbm, out_sem.at[2]))
-    outs[-1].start()
-
-    for copy in z_copies:
+
+    for k in reversed(z_order[:-1]):
+        z_copies[k].wait_recv()
+        for j in x_order:
+            x_copies[j].append(send(own(k), own(k), {"lon": at_x(j) * ny + y}))
+    core_copies = [send(af_v.at[core, x], af_v.at[core, x], partner)]
+    bg_v[...] = bias_add(3, ny, bias_waits) * (1.0 / math.sqrt(ncells))
+    for k in reversed(x_order):
+        for copy in x_copies[k]:
+            copy.wait_recv()
+        block = af_v.at[core, lax.rem(x - k + nx, nx)]
+        core_copies.append(send(block, block, partner))
+    for copy in core_copies:
         copy.wait_recv()
-    x_copies = []
-    for j in range(1, nx):
-        k = next(sem)
-        x_copies.append(push(af_v.at[core, x], af_v.at[core, x], r_send.at[k], r_recv.at[k],
-                             {"lon": at_x(j) * ny + y}))
-    for copy in x_copies:
-        copy.wait_recv()
-    k = next(sem)
-    core_copy = push(af_v.at[core], af_v.at[core], r_send.at[k], r_recv.at[k], partner)
-    core_copy.wait_recv()
+    for copy in sends:
+        copy.wait_send()
+
+
+def leave(fg_v, mlg_v, mhg_v, af_v, bias_v, fg_hbm, mlg_hbm, mhg_hbm, wg_hbm, bg_hbm,
+          wg_v, bg_v, sem):
+    copies = [
+        pltpu.make_async_copy(fg_v, fg_hbm, sem.at[0]),
+        pltpu.make_async_copy(mlg_v, mlg_hbm, sem.at[1]),
+        pltpu.make_async_copy(mhg_v, mhg_hbm, sem.at[2]),
+        pltpu.make_async_copy(wg_v, wg_hbm, sem.at[3]),
+        pltpu.make_async_copy(bg_v, bg_hbm, sem.at[4]),
+    ]
+    for copy in copies[:3]:
+        copy.start()
     for h in range(2):
         wg_v[:, h * 128 : (h + 1) * 128] = af_v[h].reshape(256, 128)
-    outs.append(pltpu.make_async_copy(wg_v, wg_hbm, out_sem.at[3]))
-    outs.append(pltpu.make_async_copy(bg_v, bg_hbm, out_sem.at[4]))
-    for copy in outs[3:]:
+        bg_v[:, h * 128 : (h + 1) * 128] = bias_v[h : h + 1]
+    for copy in copies[3:]:
         copy.start()
-    for copy in outs:
+    for copy in copies:
         copy.wait()
-    for copy in sends:
-        copy.wait_send()
 
 
 def shards(fields, cotangent, mix_low, mix_high, point_weight, point_bias):
@@ -422,7 +461,9 @@
     nx = nlon // ny
     tx = 32 // nx
     tz = tx // nz
-    messages = 2 + 2 * (nx - 1) + 2 * (nz - 1) + (ny - 1)
+    groups = 4 if nz == 8 else nz
+    messages = 2 + groups * (nx - 1) + (nx - 1) + 2 * (nz - 1) + 2 * (ny - 1)
+    messages += (nz - 1) + nz * (nx - 1) + nx
     vmem = pltpu.VMEM
     scratch = [
         vmem((cells, channels), BF16), vmem((cells, channels), BF16),
@@ -431,18 +472,16 @@
         vmem((cells, 256), BF16), vmem((channels, cells), BF16), vmem((channels, channels), BF16),
         vmem((cells, channels), BF16), vmem((cells, channels), BF16),
         vmem((256, channels), BF16), vmem((128, channels), BF16), vmem((8, channels), F32),
-        vmem((cells, channels), BF16), vmem(mix_low.shape, BF16), vmem(mix_high.shape, BF16),
-        vmem((channels, channels), F32), vmem((1, channels), F32),
         vmem((2, 4, 4, 8, channels), F32), vmem((2, 4, 4, 8, channels), F32),
         vmem((2, 4, 8, channels), F32), vmem((2, 4, 8, channels), F32),
         vmem((2, 8, channels), F32), vmem((2, 4, 8, channels), F32),
         vmem((2, 4, 8, channels), F32), vmem((2, 4, 4, 8, channels), F32),
-        vmem((2, 33, 8, 128), F32), vmem((33, 8, 128), F32),
-        vmem((nx, tx + 1, 8, 128), F32), vmem((nx, tx + 1, 8, 128), F32),
-        vmem((nz, tz + 1, 8, 128), F32), vmem((nz, tz + 1, 8, 128), F32),
-        vmem((tz + 1, 8, 128), F32), vmem((ny, tz + 1, 8, 128), F32),
-        vmem((2, nx, nz, tz, 8, 128), F32),
-        pltpu.SemaphoreType.DMA((7,)), pltpu.SemaphoreType.DMA((5,)),
+        vmem((2, 32, 8, 128), F32), vmem((32, 8, 128), F32),
+        vmem((nx - 1, nz, tz, 8, 128), F32), vmem((nx, nz, tz, 8, 128), F32),
+        vmem((nz, tz, 8, 128), F32), vmem((nz, tz, 8, 128), F32),
+        vmem((tz, 8, 128), F32), vmem((ny, tz, 8, 128), F32),
+        vmem((4, 2, 128), F32), vmem((2, 128), F32), vmem((4, max(nx, ny, nz), 2, 128), F32),
+        pltpu.SemaphoreType.DMA((7,)),
         pltpu.SemaphoreType.DMA((2, 4, 4)), pltpu.SemaphoreType.DMA((2, 4, 4)),
         pltpu.SemaphoreType.DMA((messages,)), pltpu.SemaphoreType.DMA((messages,)),
     ]
@@ -452,20 +491,41 @@
             jax.ShapeDtypeStruct((cells, channels), BF16),
             jax.ShapeDtypeStruct(mix_low.shape, BF16),
             jax.ShapeDtypeStruct(mix_high.shape, BF16),
-            jax.ShapeDtypeStruct((channels, channels), F32),
-            jax.ShapeDtypeStruct((1, channels), F32),
+            jax.ShapeDtypeStruct((2, nx, nz, tz, 8, 128), F32),
+            jax.ShapeDtypeStruct((2, 128), F32),
         ),
-        in_specs=[pl.BlockSpec(memory_space=pl.ANY)] * 7,
-        out_specs=[pl.BlockSpec(memory_space=pl.ANY)] * 5,
+        in_specs=[pl.BlockSpec(memory_space=pltpu.HBM)] * 7,
+        out_specs=[pl.BlockSpec(memory_space=vmem)] * 5,
         scratch_shapes=scratch,
         compiler_params=pltpu.CompilerParams(
             collective_id=0, has_side_effects=True, vmem_limit_bytes=32 * 1024 * 1024
         ),
         name="wavelet_block",
-    )(
-        fields.reshape(cells, channels), cotangent.reshape(cells, channels), mix_low, mix_high,
-        point_weight, point_bias.reshape(1, channels), tables,
-    )
+    )(*[
+        pltpu.with_memory_space_constraint(array, pltpu.HBM)
+        for array in (
+            fields.reshape(cells, channels), cotangent.reshape(cells, channels), mix_low, mix_high,
+            point_weight, point_bias.reshape(1, channels), tables,
+        )
+    ])
+    outs = pl.pallas_call(
+        leave,
+        out_shape=(
+            jax.ShapeDtypeStruct((cells, channels), BF16),
+            jax.ShapeDtypeStruct(mix_low.shape, BF16),
+            jax.ShapeDtypeStruct(mix_high.shape, BF16),
+            jax.ShapeDtypeStruct((channels, channels), F32),
+            jax.ShapeDtypeStruct((1, channels), F32),
+        ),
+        in_specs=[pl.BlockSpec(memory_space=vmem)] * 5,
+        out_specs=[pl.BlockSpec(memory_space=pltpu.HBM)] * 5,
+        scratch_shapes=[
+            vmem((channels, channels), F32), vmem((1, channels), F32),
+            pltpu.SemaphoreType.DMA((5,)),
+        ],
+        compiler_params=pltpu.CompilerParams(vmem_limit_bytes=16 * 1024 * 1024),
+        name="leave",
+    )(outs[0], outs[1], outs[2], outs[3].reshape(2, 32, 8, 128), outs[4])
     return (
         outs[0].reshape(fields.shape), outs[1], outs[2], outs[3], outs[4].reshape(channels),
     )

time: 71.4 us -> 61.1 us (0.86)
  local copies, waits for them, and re-layouts: 10.8 us -> 0 us
    unnamed x19 -> x0, local copies, waits for them, and re-layouts: 10.8 us -> none
    pallas_call x0 -> x1, Pallas kernels: none -> 1.27 us  [shards(): pl.pallas_call(leave, out_shape=(jax.ShapeDtypeStruct((cells, channels),...]
where the time goes in v2:
time: 61.1 us; the launch traced here: 60.9 us
  Pallas kernels  60.3 us (99%)
  between operations  0.64 us (1%)
    pallas_call x1, Pallas kernels, shards(): pl.pallas_call(functools.partial(kernel, (nlat, nlon, cells * nlat * nlon...  59 us
    pallas_call x1, Pallas kernels, shards(): pl.pallas_call(leave, out_shape=(jax.ShapeDtypeStruct((cells, channels),...  1.27 us

profile of v2, /device:TPU:1, one launch (start us, length us, event | category | flops | bytes accessed | tf_op | source)
XLA Modules:
  0.0 60.9 jit_solution(692887718268665311)
XLA Ops:
  0.6 59.0 %wavelet_block.1 = (bf16[1024,256]{1,0:T(8,128)(2,1)S(1)}, bf16[2,2,256,256]{3,2,1,0:T(8,128)(2,1)S(1)}, bf16[2,2,256,256]{3,2,1,0:T(8,128)(2,1)S(1)}, f32[2,4,8,1,8,128]{5,4,3,2,1,0:T(8,128)S(1)}, f32[2,128]{1,0:T(2,128)S(1)}) custom-call(bf16[1024,256]{1,0:T(8,128)(2,1)} %bitcast.7, bf16[1024,256]{1,0:T(8,128)(2,1)} %bitcast.8, ...), custom_call_target="tpu_custom_call" | custom-call | tf_op jit(solution)/shard_map/wavelet_block/pallas_call | solution.py:488
  59.6 1.3 %leave.1 = (bf16[1024,256]{1,0:T(8,128)(2,1)}, bf16[2,2,256,256]{3,2,1,0:T(8,128)(2,1)}, bf16[2,2,256,256]{3,2,1,0:T(8,128)(2,1)}, f32[256,256]{1,0:T(8,128)}, f32[1,256]{1,0:T(1,128)}) custom-call(bf16[1024,256]{1,0:T(8,128)(2,1)S(1)} %get-tuple-element.15.fg_v, bf16[2,2,256,256]{3,2,1,0:T(8,128)(2,1)S(1)} %get-tuple-element.16.mlg_v, ...), custom_call_target="tpu_custom_call" | custom-call | tf_op jit(solution)/shard_map/leave/pallas_call | solution.py:511

commit v3 on v2

--- a/solution.py
+++ b/solution.py
@@ -80,6 +80,7 @@
                 for f in range(2):
                     cols[block, q, f] = lons[f][k, sector : 2 * sector]
         table = np.einsum("apn,bqfm->abpqfnm", rows, cols)
+        table[:3, 3] = table[:3, 3].transpose(0, 2, 1, 3, 4, 5)
         tables.append(table.reshape(128, band * sector))
     full = np.stack(tables).astype(np.float32)
     high = full.astype(jnp.bfloat16)
@@ -87,12 +88,30 @@
     return np.concatenate([high, low], axis=1)
 
 
+def offsets():
+    steps = [(i, j) for i in range(-2, 3) for j in range(-2, 3) if (i, j) != (0, 0)]
+    return sorted(steps, key=lambda s: -(abs(s[1]) + abs(s[0]) / 2))
+
+
+def place(i, j):
+    a = 3 if abs(i) == 2 else i + 1
+    b = 3 if abs(j) == 2 else j + 1
+    start, size = 0, 8
+    if a == 3 and b == 3:
+        start, size = (4 if i < 0 else 0) + (2 if j < 0 else 0), 2
+    elif a == 3:
+        start, size = (4 if i < 0 else 0), 4
+    elif b == 3:
+        start, size = (4 if j < 0 else 0), 4
+    return a, b, pl.ds(start, size)
+
+
 def kernel(
     dims, x_hbm, cot_hbm, mixl_hbm, mixh_hbm, w_hbm, bias_hbm, k_hbm,
     fg_v, mlg_v, mhg_v, af_v, bg_v,
     x_v, cot_v, mixl_v, mixh_v, w_v, bias_v, kd_v,
     ku_v, xt_v, wt_v, ghi_v, glo_v, mm_v, ml_v, bacc_v,
-    as_v, ar_v, ss_v, sr_v, gm_v, gr_v, gs_v, gg_v,
+    as_v, ar_v, gm_v, gg_v,
     cs_v, cr_v, xs_v, xr_v, zs_v, zr_v, ys_v, yr_v,
     bs_v, bc_v, br_v,
     in_sem, h_send, h_recv, r_send, r_recv,
@@ -106,13 +125,11 @@
     core, z = lax.rem(lat, 2), lat // 2
     y, x = lax.rem(lon, ny), lon // ny
 
-    def at_lat(step):
-        return {"lat": lax.rem(lat + step + nlat, nlat)}
-
-    def at_lon(step):
-        return {"lon": lax.rem(lon + step + nlon, nlon)}
-
-    partner = {"lat": lat + 1 - 2 * core}
+    def at(i, j):
+        return (lax.rem(lat + i + nlat, nlat), lax.rem(lon + j + nlon, nlon))
+
+    other = lat + 1 - 2 * core
+    partner = {"lat": other}
 
     def at_z(k):
         return lax.rem(z + k, nz)
@@ -129,13 +146,13 @@
         (mixl_hbm, mixl_v), (mixh_hbm, mixh_v), (cot_hbm, cot_v),
     ]
     loads = [pltpu.make_async_copy(s, d, in_sem.at[i]) for i, (s, d) in enumerate(loads)]
-    for copy in loads:
+    for copy in loads[:2]:
         copy.start()
 
     barrier = pltpu.get_barrier_semaphore()
-    near = [at_lat(1), at_lat(-1), at_lon(1), at_lon(-1), at_lon(2), at_lon(-2)]
+    near = [at(i, j) for i, j in offsets()]
     near += [{"lat": at_z(k) * 2 + core} for k in range(1, nz)]
-    near += [{"lon": at_x(k) * ny + y} for k in range(1, nx)]
+    near += [(side, at_x(k) * ny + y) for k in range(1, nx) for side in (lat, other)]
     near += [{"lon": x * ny + at_y(k)} for k in range(1, ny)]
     for device in near:
         pl.semaphore_signal(barrier, inc=1, device_id=device, device_id_type=MESH)
@@ -152,77 +169,62 @@
         return copy
 
     row = lax.broadcasted_iota(jnp.int32, (8, 256), 0)
-    lower_p = row < 4
-    lower_q = lax.rem(row // 2, 2) < 1
     below = jnp.where(lat >= 2, 1.0, 0.0)
     above = jnp.where(lat + 2 < nlat, 1.0, 0.0)
-
-    def partial_lat_start(e, hi, lo):
-        if lo is None:
-            whole = jnp.dot(kd_v[...], hi, preferred_element_type=F32)
-            part = whole[:128] + whole[128:]
-        else:
-            whole = jnp.dot(kd_v[...], hi, preferred_element_type=F32)
-            part = whole[:128] + whole[128:]
+    edge_sum = jnp.where(row < 4, below, above)
+    edge_take = jnp.where(row < 4, above, below)
+
+    def swapped(tile):
+        up, down = pltpu.roll(tile, 6, 0), pltpu.roll(tile, 2, 0)
+        tile = jnp.where(row // 2 == 1, up, tile)
+        return jnp.where(row // 2 == 2, down, tile)
+
+    def partial_start(e, hi, lo):
+        whole = jnp.dot(kd_v[...], hi, preferred_element_type=F32)
+        part = whole[:128] + whole[128:]
+        if lo is not None:
             part = part + jnp.dot(kd_v[:128], lo, preferred_element_type=F32)
         as_v[e] = part.reshape(4, 4, 8, 256)
 
-    def partial_lat_send(e):
-        plan = ((0, 0, -1), (2, 1, 1), (3, 2, -2), (3, 3, 2))
-        return [
-            push(as_v.at[e, block], ar_v.at[e, slot], h_send.at[e, 0, slot],
-                 h_recv.at[e, 0, slot], at_lat(step))
-            for block, slot, step in plan
-        ]
-
-    def partial_lon(e, copies):
-        for copy in copies:
-            copy.wait_recv()
-        for tile in range(4):
-            far = jnp.where(lower_p, ar_v[e, 3, tile] * below, ar_v[e, 2, tile] * above)
-            ss_v[e, tile] = (as_v[e, 1, tile] + ar_v[e, 0, tile]) + (ar_v[e, 1, tile] + far)
-        plan = ((0, 0, -1), (2, 1, 1), (3, 2, -2), (3, 3, 2))
-        return [
-            push(ss_v.at[e, tile], sr_v.at[e, slot], h_send.at[e, 1, slot],
-                 h_recv.at[e, 1, slot], at_lon(step))
-            for tile, slot, step in plan
-        ]
+    def partial_send(e):
+        copies = []
+        for n, (i, j) in enumerate(offsets()):
+            spot = (e,) + place(i, j)
+            copies.append(push(as_v.at[spot], ar_v.at[spot], h_send.at[2 * e, n],
+                               h_recv.at[2 * e, n], at(i, j)))
+        return copies
 
     def partial_done(e, copies):
         for copy in copies:
             copy.wait_recv()
-        far = jnp.where(lower_q, sr_v[e, 3], sr_v[e, 2])
-        return (ss_v[e, 1] + sr_v[e, 0]) + (sr_v[e, 1] + far)
-
-    def spread_lon(e, tile):
-        gm_v[e] = tile
-        plan = ((0, 1), (1, -1), (2, 2), (3, -2))
-        return [
-            push(gm_v.at[e], gr_v.at[e, slot], h_send.at[e, 2, slot],
-                 h_recv.at[e, 2, slot], at_lon(step))
-            for slot, step in plan
-        ]
-
-    def spread_lat(e, copies):
-        for copy in copies:
-            copy.wait_recv()
-        gs_v[e, 0] = gr_v[e, 0]
-        gs_v[e, 1] = gm_v[e]
-        gs_v[e, 2] = gr_v[e, 1]
-        gs_v[e, 3] = jnp.where(lower_q, gr_v[e, 3], gr_v[e, 2])
-        plan = ((0, 1), (1, -1), (2, 2), (3, -2))
-        return [
-            push(gs_v.at[e], gg_v.at[e, slot], h_send.at[e, 3, slot],
-                 h_recv.at[e, 3, slot], at_lat(step))
-            for slot, step in plan
-        ]
+        total = as_v[e, 1, 1]
+        for a in range(3):
+            for b in range(3):
+                if (a, b) != (1, 1):
+                    total = total + ar_v[e, a, b]
+        far = (ar_v[e, 3, 0] + ar_v[e, 3, 1]) + (ar_v[e, 3, 2] + ar_v[e, 3, 3])
+        side = ar_v[e, 0, 3] + ar_v[e, 1, 3] + ar_v[e, 2, 3]
+        return total + far * edge_sum + swapped(side)
+
+    def spread(e, tile):
+        gm_v[e, 0] = tile
+        gm_v[e, 1] = swapped(tile)
+        gg_v[e, 1, 1] = tile
+        copies = []
+        for n, (i, j) in enumerate(offsets()):
+            a, b, rows = place(-i, -j)
+            form = 1 if b == 3 and a < 3 else 0
+            copies.append(push(gm_v.at[e, form, rows], gg_v.at[e, a, b, rows],
+                               h_send.at[2 * e + 1, n], h_recv.at[2 * e + 1, n], at(i, j)))
+        return copies
 
     def spread_done(e, copies):
         for copy in copies:
             copy.wait_recv()
-        far = jnp.where(lower_p[None], gg_v[e, 3] * above, gg_v[e, 2] * below)
-        parts = (gg_v[e, 0], gs_v[e], gg_v[e, 1], far)
-        for block, part in enumerate(parts):
+        for block in range(4):
+            part = gg_v[e, block]
+            if block == 3:
+                part = part * edge_take[None]
             part = part.reshape(32, 256)
             high = part.astype(BF16)
             low = (part - high.astype(F32)).astype(BF16)
@@ -239,9 +241,11 @@
 
     loads[0].wait()
     loads[1].wait()
-    partial_lat_start(0, x_v[...], None)
+    for copy in loads[2:]:
+        copy.start()
+    partial_start(0, x_v[...], None)
     pl.semaphore_wait(barrier, len(near))
-    copies = partial_lat_send(0)
+    copies = partial_send(0)
 
     loads[2].wait()
     loads[3].wait()
@@ -252,13 +256,11 @@
     loads[5].wait()
     loads[6].wait()
 
-    copies = partial_lon(0, copies)
     coarse = partial_done(0, copies).astype(BF16).astype(F32)
     mixed = jnp.dot(picked(coarse, 0), mixer(0), preferred_element_type=F32)
     for r in range(1, 8):
         mixed = mixed + jnp.dot(picked(coarse, r), mixer(r), preferred_element_type=F32)
-    copies = spread_lon(0, mixed)
-    copies = spread_lat(0, copies)
+    copies = spread(0, mixed)
     spread_done(0, copies)
 
     bacc_v[...] = jnp.zeros_like(bacc_v)
@@ -283,41 +285,41 @@
 
     total = jnp.dot(xt_v[...], ghi_v[...], preferred_element_type=F32)
     for h in range(2):
-        cs_v[h] = total[:, h * 128 : (h + 1) * 128].reshape(32, 8, 128)
+        cs_v[h] = total[:, h * 128 : (h + 1) * 128].reshape(nx, nz, tz, 8, 128)
     sem = iter(range(r_send.shape[0]))
 
     def send(src, dst, device):
         k = next(sem)
         return push(src, dst, r_send.at[k], r_recv.at[k], device)
 
-    core_copy = send(cs_v.at[1 - core], cr_v, partner)
+    z_order = sorted(range(nz), key=lambda k: -min(k, nz - k))
+    x_order = sorted(range(1, nx), key=lambda k: -min(k, nx - k))
+    y_order = sorted(range(1, ny), key=lambda k: -min(k, ny - k))
+    cuts = sorted({0, 1, 3, 5, nz}) if nz == 8 else range(nz + 1)
+    groups = list(zip(cuts, cuts[1:]))
+
+    core_copies = [
+        send(cs_v.at[1 - core, :, at_z(k)], cr_v.at[:, at_z(k)], partner) for k in z_order
+    ]
     bias_sum = jnp.sum(bacc_v[...], axis=0, keepdims=True)
     bs_v[0, 0:1] = bias_sum[:, :128]
     bs_v[0, 1:2] = bias_sum[:, 128:]
     bias_core = send(bs_v.at[0], bc_v, partner)
 
-    partial_lat_start(1, ghi_v[...], glo_v[...])
-    copies = partial_lat_send(1)
-
-    z_order = sorted(range(nz), key=lambda k: -min(k, nz - k))
-    x_order = sorted(range(1, nx), key=lambda k: -min(k, nx - k))
-    y_order = sorted(range(1, ny), key=lambda k: -min(k, ny - k))
-    cuts = sorted({0, 1, 3, 5, nz})
-    groups = [(i, j) for i, j in zip(cuts, cuts[1:]) if j <= nz]
-    if nz < 8:
-        groups = [(i, i + 1) for i in range(nz)]
-
-    core_copy.wait_recv()
+    partial_start(1, ghi_v[...], glo_v[...])
+    copies = partial_send(1)
+
     x_copies = []
     for start, stop in groups:
         waits = []
         for i in range(start, stop):
-            part = pl.ds((x * nz + at_z(z_order[i])) * tz, tz)
-            xr_v[x, i] = cs_v[core, part] + cr_v[part]
+            core_copies[i].wait_recv()
+            zi = at_z(z_order[i])
+            xr_v[x, i] = cs_v[core, x, zi] + cr_v[x, zi]
         for d, k in enumerate(x_order):
             for i in range(start, stop):
-                part = pl.ds((at_x(k) * nz + at_z(z_order[i])) * tz, tz)
-                xs_v[d, i] = cs_v[core, part] + cr_v[part]
+                xi, zi = at_x(k), at_z(z_order[i])
+                xs_v[d, i] = cs_v[core, xi, zi] + cr_v[xi, zi]
             span = pl.ds(start, stop - start)
             waits.append(send(xs_v.at[d, span], xr_v.at[x, span], {"lon": at_x(k) * ny + y}))
         x_copies.append(waits)
@@ -338,8 +340,6 @@
     bias_core.wait_recv()
     bias_part = bs_v[0] + bc_v[...]
     bias_waits = bias_spread(1, x_order, x, lambda k: {"lon": at_x(k) * ny + y})
-
-    copies = partial_lon(1, copies)
 
     z_copies = []
     for (start, stop), waits in zip(groups, x_copies):
@@ -365,7 +365,7 @@
         term = lax.dot_general(picked(back_rounded, r), mixer(r), (((1,), (1,)), ((), ())),
                                preferred_element_type=F32)
         pull = term if pull is None else pull + term
-    copies = spread_lon(1, pull)
+    copies = spread(1, pull)
 
     for copy in z_copies:
         copy.wait_recv()
@@ -378,8 +378,6 @@
     bias_part = bias_add(2, nz, bias_waits)
     bias_waits = bias_spread(3, y_order, y, lambda k: {"lon": x * ny + at_y(k)})
 
-    copies = spread_lat(1, copies)
-
     columns = coarse.T
     for r in range(8):
         p, q, f = r // 4, (r // 2) % 2, r % 2
@@ -393,15 +391,17 @@
         red = red + yr_v[j]
     af_v[core, x, z] = red * (1.0 / math.sqrt(ncells))
 
+    last = z_order[0]
+    sooner = list(reversed(z_order[1:]))
+
     def own(k):
         return af_v.at[core, x, lax.rem(z - k + nz, nz)]
 
     z_copies = {}
     for k in z_order[:-1]:
         z_copies[k] = send(own(0), own(0), {"lat": at_z(k) * 2 + core})
-    x_copies = {k: [] for k in x_order}
-    for k in x_order:
-        x_copies[k].append(send(own(0), own(0), {"lon": at_x(k) * ny + y}))
+    x_copies = {}
+    x_copies[0] = [send(own(0), own(0), {"lon": at_x(j) * ny + y}) for j in x_order]
 
     spread_done(1, copies)
 
@@ -415,18 +415,22 @@
 
     lax.fori_loop(0, 1024 // chunk, back_out, 0)
 
-    for k in reversed(z_order[:-1]):
+    for k in sooner[1:]:
         z_copies[k].wait_recv()
-        for j in x_order:
-            x_copies[j].append(send(own(k), own(k), {"lon": at_x(j) * ny + y}))
-    core_copies = [send(af_v.at[core, x], af_v.at[core, x], partner)]
+        x_copies[k] = [send(own(k), own(k), {"lon": at_x(j) * ny + y}) for j in x_order]
+    z_copies[last].wait_recv()
+    arrivals = [
+        send(own(last), own(last), (side, at_x(j) * ny + y))
+        for j in x_order for side in (lat, other)
+    ]
+    arrivals.append(send(own(last), own(last), partner))
     bg_v[...] = bias_add(3, ny, bias_waits) * (1.0 / math.sqrt(ncells))
-    for k in reversed(x_order):
+    for k in sooner:
         for copy in x_copies[k]:
             copy.wait_recv()
-        block = af_v.at[core, lax.rem(x - k + nx, nx)]
-        core_copies.append(send(block, block, partner))
-    for copy in core_copies:
+        column = af_v.at[core, :, lax.rem(z - k + nz, nz)]
+        arrivals.append(send(column, column, partner))
+    for copy in arrivals:
         copy.wait_recv()
     for copy in sends:
         copy.wait_send()
@@ -461,9 +465,8 @@
     nx = nlon // ny
     tx = 32 // nx
     tz = tx // nz
-    groups = 4 if nz == 8 else nz
-    messages = 2 + groups * (nx - 1) + (nx - 1) + 2 * (nz - 1) + 2 * (ny - 1)
-    messages += (nz - 1) + nz * (nx - 1) + nx
+    messages = 2 * nz + nz * (nx - 1) + (nx - 1) + 3 * (nz - 1) + 2 * (ny - 1)
+    messages += (nz + 1) * (nx - 1) + 1
     vmem = pltpu.VMEM
     scratch = [
         vmem((cells, channels), BF16), vmem((cells, channels), BF16),
@@ -473,16 +476,14 @@
         vmem((cells, channels), BF16), vmem((cells, channels), BF16),
         vmem((256, channels), BF16), vmem((128, channels), BF16), vmem((8, channels), F32),
         vmem((2, 4, 4, 8, channels), F32), vmem((2, 4, 4, 8, channels), F32),
-        vmem((2, 4, 8, channels), F32), vmem((2, 4, 8, channels), F32),
-        vmem((2, 8, channels), F32), vmem((2, 4, 8, channels), F32),
-        vmem((2, 4, 8, channels), F32), vmem((2, 4, 4, 8, channels), F32),
-        vmem((2, 32, 8, 128), F32), vmem((32, 8, 128), F32),
+        vmem((2, 2, 8, channels), F32), vmem((2, 4, 4, 8, channels), F32),
+        vmem((2, nx, nz, tz, 8, 128), F32), vmem((nx, nz, tz, 8, 128), F32),
         vmem((nx - 1, nz, tz, 8, 128), F32), vmem((nx, nz, tz, 8, 128), F32),
         vmem((nz, tz, 8, 128), F32), vmem((nz, tz, 8, 128), F32),
         vmem((tz, 8, 128), F32), vmem((ny, tz, 8, 128), F32),
         vmem((4, 2, 128), F32), vmem((2, 128), F32), vmem((4, max(nx, ny, nz), 2, 128), F32),
         pltpu.SemaphoreType.DMA((7,)),
-        pltpu.SemaphoreType.DMA((2, 4, 4)), pltpu.SemaphoreType.DMA((2, 4, 4)),
+        pltpu.SemaphoreType.DMA((4, 24)), pltpu.SemaphoreType.DMA((4, 24)),
         pltpu.SemaphoreType.DMA((messages,)), pltpu.SemaphoreType.DMA((messages,)),
     ]
     outs = pl.pallas_call(

time: 61.1 us -> 56.5 us (0.925)
  Pallas kernels: 60.3 us -> 55.7 us
    pallas_call x1, Pallas kernels: 59 us -> 54.4 us  [shards(): pl.pallas_call(functools.partial(kernel, (nlat, nlon, cells * nlat * nlon...]
where the time goes in v3:
time: 56.5 us; the launch traced here: 56.3 us
  Pallas kernels  55.7 us (99%)
  between operations  0.64 us (1%)
    pallas_call x1, Pallas kernels, shards(): pl.pallas_call(functools.partial(kernel, (nlat, nlon, cells * nlat * nlon...  54.4 us
    pallas_call x1, Pallas kernels, shards(): pl.pallas_call(leave, out_shape=(jax.ShapeDtypeStruct((cells, channels),...  1.27 us

profile of v3, /device:TPU:1, one launch (start us, length us, event | category | flops | bytes accessed | tf_op | source)
XLA Modules:
  0.0 56.3 jit_solution(11012757608169576973)
XLA Ops:
  0.6 54.4 %wavelet_block.1 = (bf16[1024,256]{1,0:T(8,128)(2,1)S(1)}, bf16[2,2,256,256]{3,2,1,0:T(8,128)(2,1)S(1)}, bf16[2,2,256,256]{3,2,1,0:T(8,128)(2,1)S(1)}, f32[2,4,8,1,8,128]{5,4,3,2,1,0:T(8,128)S(1)}, f32[2,128]{1,0:T(2,128)S(1)}) custom-call(bf16[1024,256]{1,0:T(8,128)(2,1)} %bitcast.7, bf16[1024,256]{1,0:T(8,128)(2,1)} %bitcast.8, ...), custom_call_target="tpu_custom_call" | custom-call | tf_op jit(solution)/shard_map/wavelet_block/pallas_call | solution.py:489
  55.1 1.3 %leave.1 = (bf16[1024,256]{1,0:T(8,128)(2,1)}, bf16[2,2,256,256]{3,2,1,0:T(8,128)(2,1)}, bf16[2,2,256,256]{3,2,1,0:T(8,128)(2,1)}, f32[256,256]{1,0:T(8,128)}, f32[1,256]{1,0:T(1,128)}) custom-call(bf16[1024,256]{1,0:T(8,128)(2,1)S(1)} %get-tuple-element.15.fg_v, bf16[2,2,256,256]{3,2,1,0:T(8,128)(2,1)S(1)} %get-tuple-element.16.mlg_v, ...), custom_call_target="tpu_custom_call" | custom-call | tf_op jit(solution)/shard_map/leave/pallas_call | solution.py:512

commit v4 on v3

--- a/solution.py
+++ b/solution.py
@@ -112,9 +112,9 @@
     x_v, cot_v, mixl_v, mixh_v, w_v, bias_v, kd_v,
     ku_v, xt_v, wt_v, ghi_v, glo_v, mm_v, ml_v, bacc_v,
     as_v, ar_v, gm_v, gg_v,
-    cs_v, cr_v, xs_v, xr_v, zs_v, zr_v, ys_v, yr_v,
+    cs_v, cr_v, xs_v, rr_v, ys_v, yr_v,
     bs_v, bc_v, br_v,
-    in_sem, h_send, h_recv, r_send, r_recv,
+    in_sem, h_send, h_recv, r_send, r_recv, hello,
 ):
     nlat, nlon, ncells = dims
     nz, ny = nlat // 2, min(ROW, nlon // 2)
@@ -146,8 +146,7 @@
         (mixl_hbm, mixl_v), (mixh_hbm, mixh_v), (cot_hbm, cot_v),
     ]
     loads = [pltpu.make_async_copy(s, d, in_sem.at[i]) for i, (s, d) in enumerate(loads)]
-    for copy in loads[:2]:
-        copy.start()
+    loads[0].start()
 
     barrier = pltpu.get_barrier_semaphore()
     near = [at(i, j) for i, j in offsets()]
@@ -156,6 +155,7 @@
     near += [{"lon": x * ny + at_y(k)} for k in range(1, ny)]
     for device in near:
         pl.semaphore_signal(barrier, inc=1, device_id=device, device_id_type=MESH)
+    loads[1].start()
 
     sends = []
 
@@ -246,6 +246,9 @@
     partial_start(0, x_v[...], None)
     pl.semaphore_wait(barrier, len(near))
     copies = partial_send(0)
+    for k in range(1, nz):
+        pl.semaphore_signal(hello, inc=1, device_id={"lat": at_z(k) * 2 + core},
+                            device_id_type=MESH)
 
     loads[2].wait()
     loads[3].wait()
@@ -295,9 +298,6 @@
     z_order = sorted(range(nz), key=lambda k: -min(k, nz - k))
     x_order = sorted(range(1, nx), key=lambda k: -min(k, nx - k))
     y_order = sorted(range(1, ny), key=lambda k: -min(k, ny - k))
-    cuts = sorted({0, 1, 3, 5, nz}) if nz == 8 else range(nz + 1)
-    groups = list(zip(cuts, cuts[1:]))
-
     core_copies = [
         send(cs_v.at[1 - core, :, at_z(k)], cr_v.at[:, at_z(k)], partner) for k in z_order
     ]
@@ -309,20 +309,19 @@
     partial_start(1, ghi_v[...], glo_v[...])
     copies = partial_send(1)
 
-    x_copies = []
-    for start, stop in groups:
-        waits = []
-        for i in range(start, stop):
-            core_copies[i].wait_recv()
-            zi = at_z(z_order[i])
-            xr_v[x, i] = cs_v[core, x, zi] + cr_v[x, zi]
-        for d, k in enumerate(x_order):
-            for i in range(start, stop):
-                xi, zi = at_x(k), at_z(z_order[i])
-                xs_v[d, i] = cs_v[core, xi, zi] + cr_v[xi, zi]
-            span = pl.ds(start, stop - start)
-            waits.append(send(xs_v.at[d, span], xr_v.at[x, span], {"lon": at_x(k) * ny + y}))
-        x_copies.append(waits)
+    pl.semaphore_wait(hello, nz - 1)
+    own_copies = []
+    for n, k in enumerate(z_order):
+        core_copies[n].wait_recv()
+        zi = at_z(k)
+        for j in x_order + [0]:
+            xi = at_x(j)
+            part = cs_v[core, xi, zi] + cr_v[xi, zi]
+            if j == 0 and k == 0:
+                rr_v[x, z] = part
+            else:
+                xs_v[j, k] = part
+                own_copies.append(send(xs_v.at[j, k], rr_v.at[x, z], (zi * 2 + core, xi * ny + y)))
 
     def bias_spread(i, order, slot, device):
         bs_v[i] = bias_part
@@ -341,24 +340,9 @@
     bias_part = bs_v[0] + bc_v[...]
     bias_waits = bias_spread(1, x_order, x, lambda k: {"lon": at_x(k) * ny + y})
 
-    z_copies = []
-    for (start, stop), waits in zip(groups, x_copies):
-        for copy in waits:
-            copy.wait_recv()
-        for i in range(start, stop):
-            k = z_order[i]
-            part = xr_v[0, i]
-            for j in range(1, nx):
-                part = part + xr_v[j, i]
-            if k == 0:
-                zr_v[z] = part
-            else:
-                zs_v[i] = part
-                z_copies.append(send(zs_v.at[i], zr_v.at[z], {"lat": at_z(k) * 2 + core}))
+    back = partial_done(1, copies)
     bias_part = bias_add(1, nx, bias_waits)
     bias_waits = bias_spread(2, z_order[:-1], z, lambda k: {"lat": at_z(k) * 2 + core})
-
-    back = partial_done(1, copies)
     back_rounded = back.astype(BF16).astype(F32)
     pull = None
     for r in range(8):
@@ -367,11 +351,17 @@
         pull = term if pull is None else pull + term
     copies = spread(1, pull)
 
-    for copy in z_copies:
+    for copy in own_copies:
         copy.wait_recv()
-    red = zr_v[0]
-    for j in range(1, nz):
-        red = red + zr_v[j]
+    columns = []
+    for i in range(nx):
+        red = rr_v[i, 0]
+        for j in range(1, nz):
+            red = red + rr_v[i, j]
+        columns.append(red)
+    red = columns[0]
+    for column in columns[1:]:
+        red = red + column
     ys_v[...] = red
     yr_v[y] = red
     y_copies = [send(ys_v, yr_v.at[y], {"lon": x * ny + at_y(k)}) for k in y_order]
@@ -392,16 +382,16 @@
     af_v[core, x, z] = red * (1.0 / math.sqrt(ncells))
 
     last = z_order[0]
-    sooner = list(reversed(z_order[1:]))
-
-    def own(k):
-        return af_v.at[core, x, lax.rem(z - k + nz, nz)]
-
-    z_copies = {}
-    for k in z_order[:-1]:
-        z_copies[k] = send(own(0), own(0), {"lat": at_z(k) * 2 + core})
+    tile = af_v.at[core, x, z]
+    arrivals = [
+        send(tile, tile, (at_z(last) * 2 + 1 - core, at_x(j) * ny + y)) for j in x_order + [0]
+    ]
     x_copies = {}
-    x_copies[0] = [send(own(0), own(0), {"lon": at_x(j) * ny + y}) for j in x_order]
+    for k in z_order:
+        x_copies[k] = [
+            send(tile, tile, (at_z(k) * 2 + core, at_x(j) * ny + y))
+            for j in x_order + [0] if (j, k) != (0, 0)
+        ]
 
     spread_done(1, copies)
 
@@ -415,21 +405,13 @@
 
     lax.fori_loop(0, 1024 // chunk, back_out, 0)
 
-    for k in sooner[1:]:
-        z_copies[k].wait_recv()
-        x_copies[k] = [send(own(k), own(k), {"lon": at_x(j) * ny + y}) for j in x_order]
-    z_copies[last].wait_recv()
-    arrivals = [
-        send(own(last), own(last), (side, at_x(j) * ny + y))
-        for j in x_order for side in (lat, other)
-    ]
-    arrivals.append(send(own(last), own(last), partner))
-    bg_v[...] = bias_add(3, ny, bias_waits) * (1.0 / math.sqrt(ncells))
-    for k in sooner:
+    for k in reversed(z_order[1:]):
         for copy in x_copies[k]:
             copy.wait_recv()
         column = af_v.at[core, :, lax.rem(z - k + nz, nz)]
         arrivals.append(send(column, column, partner))
+    bg_v[...] = bias_add(3, ny, bias_waits) * (1.0 / math.sqrt(ncells))
+    arrivals += x_copies[last]
     for copy in arrivals:
         copy.wait_recv()
     for copy in sends:
@@ -465,8 +447,7 @@
     nx = nlon // ny
     tx = 32 // nx
     tz = tx // nz
-    messages = 2 * nz + nz * (nx - 1) + (nx - 1) + 3 * (nz - 1) + 2 * (ny - 1)
-    messages += (nz + 1) * (nx - 1) + 1
+    messages = 2 * (nx * nz - 1) + nx + 2 * nz + (nx - 1) + (nz - 1) + 2 * (ny - 1)
     vmem = pltpu.VMEM
     scratch = [
         vmem((cells, channels), BF16), vmem((cells, channels), BF16),
@@ -478,13 +459,13 @@
         vmem((2, 4, 4, 8, channels), F32), vmem((2, 4, 4, 8, channels), F32),
         vmem((2, 2, 8, channels), F32), vmem((2, 4, 4, 8, channels), F32),
         vmem((2, nx, nz, tz, 8, 128), F32), vmem((nx, nz, tz, 8, 128), F32),
-        vmem((nx - 1, nz, tz, 8, 128), F32), vmem((nx, nz, tz, 8, 128), F32),
-        vmem((nz, tz, 8, 128), F32), vmem((nz, tz, 8, 128), F32),
+        vmem((nx, nz, tz, 8, 128), F32), vmem((nx, nz, tz, 8, 128), F32),
         vmem((tz, 8, 128), F32), vmem((ny, tz, 8, 128), F32),
         vmem((4, 2, 128), F32), vmem((2, 128), F32), vmem((4, max(nx, ny, nz), 2, 128), F32),
         pltpu.SemaphoreType.DMA((7,)),
         pltpu.SemaphoreType.DMA((4, 24)), pltpu.SemaphoreType.DMA((4, 24)),
         pltpu.SemaphoreType.DMA((messages,)), pltpu.SemaphoreType.DMA((messages,)),
+        pltpu.SemaphoreType.REGULAR,
     ]
     outs = pl.pallas_call(
         functools.partial(kernel, (nlat, nlon, cells * nlat * nlon)),

time: 56.5 us -> 55.2 us (0.977)
  Pallas kernels: 55.7 us -> 54.4 us
    pallas_call x1, Pallas kernels: 54.4 us -> 53.1 us  [shards(): pl.pallas_call(functools.partial(kernel, (nlat, nlon, cells * nlat * nlon...]
where the time goes in v4:
time: 55.2 us; the launch traced here: 55.1 us
  Pallas kernels  54.4 us (99%)
  between operations  0.64 us (1%)
    pallas_call x1, Pallas kernels, shards(): pl.pallas_call(functools.partial(kernel, (nlat, nlon, cells * nlat * nlon...  53.1 us
    pallas_call x1, Pallas kernels, shards(): pl.pallas_call(leave, out_shape=(jax.ShapeDtypeStruct((cells, channels),...  1.27 us

profile of v4, /device:TPU:1, one launch (start us, length us, event | category | flops | bytes accessed | tf_op | source)
XLA Modules:
  0.0 55.1 jit_solution(3798776096798457942)
XLA Ops:
  0.6 53.1 %wavelet_block.1 = (bf16[1024,256]{1,0:T(8,128)(2,1)S(1)}, bf16[2,2,256,256]{3,2,1,0:T(8,128)(2,1)S(1)}, bf16[2,2,256,256]{3,2,1,0:T(8,128)(2,1)S(1)}, f32[2,4,8,1,8,128]{5,4,3,2,1,0:T(8,128)S(1)}, f32[2,128]{1,0:T(2,128)S(1)}) custom-call(bf16[1024,256]{1,0:T(8,128)(2,1)} %bitcast.7, bf16[1024,256]{1,0:T(8,128)(2,1)} %bitcast.8, ...), custom_call_target="tpu_custom_call" | custom-call | tf_op jit(solution)/shard_map/wavelet_block/pallas_call | solution.py:470
  53.8 1.3 %leave.1 = (bf16[1024,256]{1,0:T(8,128)(2,1)}, bf16[2,2,256,256]{3,2,1,0:T(8,128)(2,1)}, bf16[2,2,256,256]{3,2,1,0:T(8,128)(2,1)}, f32[256,256]{1,0:T(8,128)}, f32[1,256]{1,0:T(1,128)}) custom-call(bf16[1024,256]{1,0:T(8,128)(2,1)S(1)} %get-tuple-element.15.fg_v, bf16[2,2,256,256]{3,2,1,0:T(8,128)(2,1)S(1)} %get-tuple-element.16.mlg_v, ...), custom_call_target="tpu_custom_call" | custom-call | tf_op jit(solution)/shard_map/leave/pallas_call | solution.py:493

commit v5 on v4

--- a/solution.py
+++ b/solution.py
@@ -307,7 +307,6 @@
     bias_core = send(bs_v.at[0], bc_v, partner)
 
     partial_start(1, ghi_v[...], glo_v[...])
-    copies = partial_send(1)
 
     pl.semaphore_wait(hello, nz - 1)
     own_copies = []
@@ -323,6 +322,8 @@
                 xs_v[j, k] = part
                 own_copies.append(send(xs_v.at[j, k], rr_v.at[x, z], (zi * 2 + core, xi * ny + y)))
 
+    copies = partial_send(1)
+
     def bias_spread(i, order, slot, device):
         bs_v[i] = bias_part
         br_v[i, slot] = bias_part
@@ -339,17 +340,6 @@
     bias_core.wait_recv()
     bias_part = bs_v[0] + bc_v[...]
     bias_waits = bias_spread(1, x_order, x, lambda k: {"lon": at_x(k) * ny + y})
-
-    back = partial_done(1, copies)
-    bias_part = bias_add(1, nx, bias_waits)
-    bias_waits = bias_spread(2, z_order[:-1], z, lambda k: {"lat": at_z(k) * 2 + core})
-    back_rounded = back.astype(BF16).astype(F32)
-    pull = None
-    for r in range(8):
-        term = lax.dot_general(picked(back_rounded, r), mixer(r), (((1,), (1,)), ((), ())),
-                               preferred_element_type=F32)
-        pull = term if pull is None else pull + term
-    copies = spread(1, pull)
 
     for copy in own_copies:
         copy.wait_recv()
@@ -365,8 +355,16 @@
     ys_v[...] = red
     yr_v[y] = red
     y_copies = [send(ys_v, yr_v.at[y], {"lon": x * ny + at_y(k)}) for k in y_order]
-    bias_part = bias_add(2, nz, bias_waits)
-    bias_waits = bias_spread(3, y_order, y, lambda k: {"lon": x * ny + at_y(k)})
+    back = partial_done(1, copies)
+    bias_part = bias_add(1, nx, bias_waits)
+    bias_waits = bias_spread(2, z_order[:-1], z, lambda k: {"lat": at_z(k) * 2 + core})
+    back_rounded = back.astype(BF16).astype(F32)
+    pull = None
+    for r in range(8):
+        term = lax.dot_general(picked(back_rounded, r), mixer(r), (((1,), (1,)), ((), ())),
+                               preferred_element_type=F32)
+        pull = term if pull is None else pull + term
+    copies = spread(1, pull)
 
     columns = coarse.T
     for r in range(8):
@@ -392,6 +390,9 @@
             send(tile, tile, (at_z(k) * 2 + core, at_x(j) * ny + y))
             for j in x_order + [0] if (j, k) != (0, 0)
         ]
+
+    bias_part = bias_add(2, nz, bias_waits)
+    bias_waits = bias_spread(3, y_order, y, lambda k: {"lon": x * ny + at_y(k)})
 
     spread_done(1, copies)
 

time: 55.2 us -> 54.5 us (0.987)
  Pallas kernels: 54.4 us -> 53.7 us
    pallas_call x1, Pallas kernels: 53.1 us -> 52.4 us  [shards(): pl.pallas_call(functools.partial(kernel, (nlat, nlon, cells * nlat * nlon...]
where the time goes in v5:
time: 54.5 us; the launch traced here: 54.3 us
  Pallas kernels  53.7 us (99%)
  between operations  0.64 us (1%)
    pallas_call x1, Pallas kernels, shards(): pl.pallas_call(functools.partial(kernel, (nlat, nlon, cells * nlat * nlon...  52.4 us
    pallas_call x1, Pallas kernels, shards(): pl.pallas_call(leave, out_shape=(jax.ShapeDtypeStruct((cells, channels),...  1.27 us

profile of v5, /device:TPU:1, one launch (start us, length us, event | category | flops | bytes accessed | tf_op | source)
XLA Modules:
  0.0 54.3 jit_solution(16657946652766666736)
XLA Ops:
  0.6 52.4 %wavelet_block.1 = (bf16[1024,256]{1,0:T(8,128)(2,1)S(1)}, bf16[2,2,256,256]{3,2,1,0:T(8,128)(2,1)S(1)}, bf16[2,2,256,256]{3,2,1,0:T(8,128)(2,1)S(1)}, f32[2,4,8,1,8,128]{5,4,3,2,1,0:T(8,128)S(1)}, f32[2,128]{1,0:T(2,128)S(1)}) custom-call(bf16[1024,256]{1,0:T(8,128)(2,1)} %bitcast.7, bf16[1024,256]{1,0:T(8,128)(2,1)} %bitcast.8, ...), custom_call_target="tpu_custom_call" | custom-call | tf_op jit(solution)/shard_map/wavelet_block/pallas_call | solution.py:471
  53.0 1.3 %leave.1 = (bf16[1024,256]{1,0:T(8,128)(2,1)}, bf16[2,2,256,256]{3,2,1,0:T(8,128)(2,1)}, bf16[2,2,256,256]{3,2,1,0:T(8,128)(2,1)}, f32[256,256]{1,0:T(8,128)}, f32[1,256]{1,0:T(1,128)}) custom-call(bf16[1024,256]{1,0:T(8,128)(2,1)S(1)} %get-tuple-element.15.fg_v, bf16[2,2,256,256]{3,2,1,0:T(8,128)(2,1)S(1)} %get-tuple-element.16.mlg_v, ...), custom_call_target="tpu_custom_call" | custom-call | tf_op jit(solution)/shard_map/leave/pallas_call | solution.py:494

commit v6 on v5

--- a/solution.py
+++ b/solution.py
@@ -269,26 +269,29 @@
     bacc_v[...] = jnp.zeros_like(bacc_v)
     chunk = 256
 
-    def gate(i, carry):
-        rows = pl.ds(pl.multiple_of(i * chunk, chunk), chunk)
-        pre = jnp.dot(ku_v[rows, :], mm_v[...], preferred_element_type=F32)
-        pre = pre + jnp.dot(ku_v[rows, :128], ml_v[...], preferred_element_type=F32)
-        pre = pre + jnp.dot(x_v[rows, :], w_v[...], preferred_element_type=F32)
-        pre = pre + bias_v[...]
-        cdf = 0.5 * (1.0 + lax.erf(pre * (1.0 / math.sqrt(2.0))))
-        pdf = jnp.exp(-0.5 * pre * pre) * (1.0 / math.sqrt(2.0 * math.pi))
-        grad = cot_v[rows, :].astype(F32) * (cdf + pre * pdf)
-        high = grad.astype(BF16)
-        ghi_v[rows, :] = high
-        glo_v[rows, :] = (grad - high.astype(F32)).astype(BF16)
-        bacc_v[...] += jnp.sum(grad.reshape(chunk // 8, 8, 256), axis=0)
-        return carry
-
-    lax.fori_loop(0, 1024 // chunk, gate, 0)
-
-    total = jnp.dot(xt_v[...], ghi_v[...], preferred_element_type=F32)
-    for h in range(2):
-        cs_v[h] = total[:, h * 128 : (h + 1) * 128].reshape(nx, nz, tz, 8, 128)
+    def gate_half(h):
+        lane = pl.ds(pl.multiple_of(h * 128, 128), 128)
+
+        def gate(i, carry):
+            rows = pl.ds(pl.multiple_of(i * chunk, chunk), chunk)
+            pre = jnp.dot(ku_v[rows, :], mm_v[:, lane], preferred_element_type=F32)
+            pre = pre + jnp.dot(ku_v[rows, :128], ml_v[:, lane], preferred_element_type=F32)
+            pre = pre + jnp.dot(x_v[rows, :], w_v[:, lane], preferred_element_type=F32)
+            pre = pre + bias_v[:, lane]
+            cdf = 0.5 * (1.0 + lax.erf(pre * (1.0 / math.sqrt(2.0))))
+            pdf = jnp.exp(-0.5 * pre * pre) * (1.0 / math.sqrt(2.0 * math.pi))
+            grad = cot_v[rows, lane].astype(F32) * (cdf + pre * pdf)
+            high = grad.astype(BF16)
+            ghi_v[rows, lane] = high
+            glo_v[rows, lane] = (grad - high.astype(F32)).astype(BF16)
+            bacc_v[:, lane] += jnp.sum(grad.reshape(chunk // 8, 8, 128), axis=0)
+            return carry
+
+        lax.fori_loop(0, 1024 // chunk, gate, 0)
+        total = jnp.dot(xt_v[...], ghi_v[:, lane], preferred_element_type=F32)
+        cs_v[h] = total.reshape(nx, nz, tz, 8, 128)
+
+    gate_half(1 - core)
     sem = iter(range(r_send.shape[0]))
 
     def send(src, dst, device):
@@ -301,12 +304,12 @@
     core_copies = [
         send(cs_v.at[1 - core, :, at_z(k)], cr_v.at[:, at_z(k)], partner) for k in z_order
     ]
+    gate_half(core)
     bias_sum = jnp.sum(bacc_v[...], axis=0, keepdims=True)
     bs_v[0, 0:1] = bias_sum[:, :128]
     bs_v[0, 1:2] = bias_sum[:, 128:]
     bias_core = send(bs_v.at[0], bc_v, partner)
 
-    partial_start(1, ghi_v[...], glo_v[...])
 
     pl.semaphore_wait(hello, nz - 1)
     own_copies = []
@@ -322,6 +325,7 @@
                 xs_v[j, k] = part
                 own_copies.append(send(xs_v.at[j, k], rr_v.at[x, z], (zi * 2 + core, xi * ny + y)))
 
+    partial_start(1, ghi_v[...], glo_v[...])
     copies = partial_send(1)
 
     def bias_spread(i, order, slot, device):

time: 54.5 us -> 54 us (level)
  no operation moved by 1% of the time
where the time goes in v6:
time: 54 us; the launch traced here: 53.8 us
  Pallas kernels  53.2 us (99%)
  between operations  0.64 us (1%)
    pallas_call x1, Pallas kernels, shards(): pl.pallas_call(functools.partial(kernel, (nlat, nlon, cells * nlat * nlon...  51.9 us
    pallas_call x1, Pallas kernels, shards(): pl.pallas_call(leave, out_shape=(jax.ShapeDtypeStruct((cells, channels),...  1.27 us

profile of v6, /device:TPU:1, one launch (start us, length us, event | category | flops | bytes accessed | tf_op | source)
XLA Modules:
  0.0 53.8 jit_solution(8981986406661128250)
XLA Ops:
  0.6 51.9 %wavelet_block.1 = (bf16[1024,256]{1,0:T(8,128)(2,1)S(1)}, bf16[2,2,256,256]{3,2,1,0:T(8,128)(2,1)S(1)}, bf16[2,2,256,256]{3,2,1,0:T(8,128)(2,1)S(1)}, f32[2,4,8,1,8,128]{5,4,3,2,1,0:T(8,128)S(1)}, f32[2,128]{1,0:T(2,128)S(1)}) custom-call(bf16[1024,256]{1,0:T(8,128)(2,1)} %bitcast.7, bf16[1024,256]{1,0:T(8,128)(2,1)} %bitcast.8, ...), custom_call_target="tpu_custom_call" | custom-call | tf_op jit(solution)/shard_map/wavelet_block/pallas_call | solution.py:475
  52.5 1.3 %leave.1 = (bf16[1024,256]{1,0:T(8,128)(2,1)}, bf16[2,2,256,256]{3,2,1,0:T(8,128)(2,1)}, bf16[2,2,256,256]{3,2,1,0:T(8,128)(2,1)}, f32[256,256]{1,0:T(8,128)}, f32[1,256]{1,0:T(1,128)}) custom-call(bf16[1024,256]{1,0:T(8,128)(2,1)S(1)} %get-tuple-element.15.fg_v, bf16[2,2,256,256]{3,2,1,0:T(8,128)(2,1)S(1)} %get-tuple-element.16.mlg_v, ...), custom_call_target="tpu_custom_call" | custom-call | tf_op jit(solution)/shard_map/leave/pallas_call | solution.py:498

commit v7 on v6

--- a/solution.py
+++ b/solution.py
@@ -383,10 +383,11 @@
         red = red + yr_v[j]
     af_v[core, x, z] = red * (1.0 / math.sqrt(ncells))
 
-    last = z_order[0]
+    late = [k for k in z_order if min(k, nz - k) > 2 or k == z_order[0]]
     tile = af_v.at[core, x, z]
     arrivals = [
-        send(tile, tile, (at_z(last) * 2 + 1 - core, at_x(j) * ny + y)) for j in x_order + [0]
+        send(tile, tile, (at_z(k) * 2 + 1 - core, at_x(j) * ny + y))
+        for k in late for j in x_order + [0]
     ]
     x_copies = {}
     for k in z_order:
@@ -410,13 +411,14 @@
 
     lax.fori_loop(0, 1024 // chunk, back_out, 0)
 
-    for k in reversed(z_order[1:]):
+    for k in reversed(z_order[len(late):]):
         for copy in x_copies[k]:
             copy.wait_recv()
         column = af_v.at[core, :, lax.rem(z - k + nz, nz)]
         arrivals.append(send(column, column, partner))
     bg_v[...] = bias_add(3, ny, bias_waits) * (1.0 / math.sqrt(ncells))
-    arrivals += x_copies[last]
+    for k in late:
+        arrivals += x_copies[k]
     for copy in arrivals:
         copy.wait_recv()
     for copy in sends:
@@ -452,7 +454,7 @@
     nx = nlon // ny
     tx = 32 // nx
     tz = tx // nz
-    messages = 2 * (nx * nz - 1) + nx + 2 * nz + (nx - 1) + (nz - 1) + 2 * (ny - 1)
+    messages = 2 * (nx * nz - 1) + 3 * nx + 2 * nz + (nx - 1) + (nz - 1) + 2 * (ny - 1)
     vmem = pltpu.VMEM
     scratch = [
         vmem((cells, channels), BF16), vmem((cells, channels), BF16),

time: 54 us -> 54.9 us (1.017)
  Pallas kernels: 53.2 us -> 54.1 us
    pallas_call x1, Pallas kernels: 51.9 us -> 52.8 us  [shards(): pl.pallas_call(functools.partial(kernel, (nlat, nlon, cells * nlat * nlon...]
where the time goes in v7:
time: 54.9 us; the launch traced here: 54.7 us
  Pallas kernels  54.1 us (99%)
  between operations  0.64 us (1%)
    pallas_call x1, Pallas kernels, shards(): pl.pallas_call(functools.partial(kernel, (nlat, nlon, cells * nlat * nlon...  52.8 us
    pallas_call x1, Pallas kernels, shards(): pl.pallas_call(leave, out_shape=(jax.ShapeDtypeStruct((cells, channels),...  1.27 us

profile of v7, /device:TPU:1, one launch (start us, length us, event | category | flops | bytes accessed | tf_op | source)
XLA Modules:
  0.0 54.7 jit_solution(6190343913469368272)
XLA Ops:
  0.6 52.8 %wavelet_block.1 = (bf16[1024,256]{1,0:T(8,128)(2,1)S(1)}, bf16[2,2,256,256]{3,2,1,0:T(8,128)(2,1)S(1)}, bf16[2,2,256,256]{3,2,1,0:T(8,128)(2,1)S(1)}, f32[2,4,8,1,8,128]{5,4,3,2,1,0:T(8,128)S(1)}, f32[2,128]{1,0:T(2,128)S(1)}) custom-call(bf16[1024,256]{1,0:T(8,128)(2,1)} %bitcast.7, bf16[1024,256]{1,0:T(8,128)(2,1)} %bitcast.8, ...), custom_call_target="tpu_custom_call" | custom-call | tf_op jit(solution)/shard_map/wavelet_block/pallas_call | solution.py:477
  53.5 1.3 %leave.1 = (bf16[1024,256]{1,0:T(8,128)(2,1)}, bf16[2,2,256,256]{3,2,1,0:T(8,128)(2,1)}, bf16[2,2,256,256]{3,2,1,0:T(8,128)(2,1)}, f32[256,256]{1,0:T(8,128)}, f32[1,256]{1,0:T(1,128)}) custom-call(bf16[1024,256]{1,0:T(8,128)(2,1)S(1)} %get-tuple-element.15.fg_v, bf16[2,2,256,256]{3,2,1,0:T(8,128)(2,1)S(1)} %get-tuple-element.16.mlg_v, ...), custom_call_target="tpu_custom_call" | custom-call | tf_op jit(solution)/shard_map/leave/pallas_call | solution.py:500
